TPU v7x, 256 devices: a whole 4x4x8 slice. The times are simulated.
256 devices in a mesh: seq: 8 (over y, core), exp: 32 (over x, z).
Axes of the slice: x: 4, y: 4, z: 8, core: 2. Of those that a mesh axis runs over, the one named last changes fastest.
Arguments:
- layer_input: bfloat16 [32, 2048, 2048], P('exp', 'seq'), may hold values from -6 to 6
- queries: bfloat16 [32, 2048, 2048], P('exp', 'seq'), may hold values from -6 to 6
- keys_in: bfloat16 [32, 2048, 2048], P('exp', 'seq'), may hold values from -0.59765625 to 0.59765625
- values_in: bfloat16 [32, 2048, 2048], P('exp', 'seq'), may hold values from -6 to 6
- decay_rate: float32 [32, 2048, 16], P('exp', 'seq'), as said below
- attn_gain: float32 [2048], replicated, may hold values from 0.25 to 1.75
- norm_gain: float32 [2048], replicated, may hold values from 0.25 to 1.75
- expert_ids: int32 [32, 2048, 2], P('exp', 'seq'), may hold values from 0 to 31, all different within a row; in each aligned block of 256 rows (0 to 255, 256 to 511, ..., all dimensions but the last counted through in order) at most 24 rows name the same one
- gate_levels: int32 [32, 2048, 2], P('exp', 'seq'), may hold values from 1 to 256
- w_gate: bfloat16 [32, 2048, 768], P('exp'), may hold values from -0.125 to 0.125
- w_up: bfloat16 [32, 2048, 768], P('exp'), may hold values from -0.125 to 0.125
- w_down: bfloat16 [32, 768, 2048], P('exp'), may hold values from -0.21875 to 0.21875
Outputs:
- layer_out: bfloat16 [32, 2048, 2048], P('exp', 'seq')
Inputs may be any that keep to these rules, and one draw needn't show every extreme that they name: `expert_ids`: each token names 2 different experts. Among the 256 positions of one device, no expert is named by more than 24 routes, a bound that some block reaches. `decay_rate`: every entry is positive.
All inputs are finite; a program needn't handle non-finite values.
Results may differ from a plain program's by a relative error of at most 0.01.
Values may be sent and summed in bfloat16 or wider, within the bound.
No kernel may reach another device: no remote copies, remote signals or barrier semaphores. Data moves between devices by JAX's collectives and lax.ppermute only.
A program may use at most 128 MiB of HBM per device.

v0:
```python
import jax
import jax.numpy as jnp
from jax import lax
from jax.sharding import PartitionSpec as P


def prefix(shard, axis, join, neutral):
    place = lax.axis_index(axis)
    gathered = jax.tree.map(
        lambda a, kind: lax.all_gather(a.astype(kind), axis), shard, (jnp.bfloat16, jnp.bfloat16)
    )
    state = jax.tree.map(lambda a, e: jnp.zeros_like(a) + jnp.asarray(e, a.dtype), shard, neutral)

    def one(hop, state):
        return join(
            state,
            jax.tree.map(
                lambda a, own: lax.dynamic_index_in_dim(a, hop, 0, False).astype(own.dtype),
                gathered,
                shard,
            ),
        )

    return lax.fori_loop(0, place, one, state)


def expert_rows(slot_block, gate_weight, up_weight, down_weight):
    row_width = slot_block.shape[2]
    flat_rows = slot_block.reshape(-1, row_width)
    gate_part = jnp.dot(flat_rows, gate_weight, preferred_element_type=jnp.float32)
    up_part = jnp.dot(flat_rows, up_weight, preferred_element_type=jnp.float32)
    activation = (jax.nn.silu(gate_part) * up_part).astype(jnp.bfloat16)
    result = jnp.dot(activation, down_weight, preferred_element_type=jnp.float32).astype(
        jnp.bfloat16
    )
    return result.reshape(slot_block.shape)


def per_device(
    layer_input,
    queries,
    keys_in,
    values_in,
    decay_rate,
    attn_gain,
    norm_gain,
    expert_ids,
    gate_levels,
    w_gate,
    w_up,
    w_down,
):
    block_len = layer_input.shape[1]
    row_width = layer_input.shape[2]
    head_count = decay_rate.shape[2]
    head_dim = row_width // head_count
    top_count = expert_ids.shape[2]
    query_heads = queries[0].reshape(block_len, head_count, head_dim)
    key_heads = keys_in[0].reshape(block_len, head_count, head_dim)
    value_heads = values_in[0].reshape(block_len, head_count, head_dim)
    cumulative = -jnp.cumsum(decay_rate[0], axis=0)
    block_total = cumulative[-1]
    key_weighted = (
        key_heads.astype(jnp.float32) * jnp.exp(block_total[None, :] - cumulative)[:, :, None]
    )
    contrib = jnp.einsum(
        "thd,the->hde",
        key_weighted,
        value_heads.astype(jnp.float32),
        precision=lax.Precision.HIGHEST,
    )

    def combine(earlier, later_part):
        return (
            earlier[0] + later_part[0],
            jnp.exp(later_part[0])[:, None, None] * earlier[1] + later_part[1],
        )

    logs_before, carried = prefix(
        (block_total, contrib),
        "seq",
        combine,
        (jnp.zeros_like(block_total), jnp.zeros_like(contrib)),
    )
    scores = jnp.einsum("thd,shd->hts", query_heads, key_heads, preferred_element_type=jnp.float32)
    cum_heads = cumulative.T
    log_gap = cum_heads[:, :, None] - cum_heads[:, None, :]
    causal = (jnp.arange(block_len)[:, None] >= jnp.arange(block_len)[None, :])[None]
    weights = jnp.where(causal, jnp.exp(jnp.minimum(log_gap, 0.0)), 0.0)
    attn_probs = (scores * weights).astype(jnp.bfloat16)
    intra_part = jnp.einsum(
        "hts,shd->thd", attn_probs, value_heads, preferred_element_type=jnp.float32
    )
    inter_part = jnp.exp(cumulative)[:, :, None] * jnp.einsum(
        "thd,hde->the", query_heads.astype(jnp.float32), carried, precision=lax.Precision.HIGHEST
    )
    raw_attn = intra_part + inter_part
    normed_heads = raw_attn / jnp.sqrt(
        jnp.mean(raw_attn * raw_attn, axis=-1, keepdims=True) + 1e-06
    )
    h_res = (
        layer_input[0].astype(jnp.float32) + normed_heads.reshape(block_len, row_width) * attn_gain
    )
    normed = (
        norm_gain * h_res / jnp.sqrt(jnp.mean(h_res * h_res, axis=-1, keepdims=True) + 1e-06)
    ).astype(jnp.bfloat16)
    owners = lax.axis_size("exp")
    capacity = 3 * block_len // owners
    flat_ids = expert_ids[0].reshape(-1)
    onehot = (flat_ids[:, None] == jnp.arange(owners, dtype=jnp.int32)[None, :]).astype(jnp.int32)
    slot_rank = jnp.sum(jnp.cumsum(onehot, axis=0) * onehot, axis=1) - 1
    position = flat_ids * capacity + slot_rank
    routed = jnp.repeat(normed, top_count, axis=0)
    send_rows = jnp.zeros((owners * capacity, row_width), jnp.bfloat16).at[position].set(routed)
    send_rows = send_rows.reshape(owners, capacity, row_width)
    expert_done = expert_rows(
        lax.all_to_all(send_rows, "exp", split_axis=0, concat_axis=0, tiled=True),
        w_gate[0],
        w_up[0],
        w_down[0],
    )
    returned = lax.all_to_all(expert_done, "exp", split_axis=0, concat_axis=0, tiled=True)
    picked = returned.reshape(owners * capacity, row_width)[position]
    gate_scale = gate_levels[0].reshape(-1).astype(jnp.float32) / 256.0
    moe_out = jnp.sum(
        (picked.astype(jnp.float32) * gate_scale[:, None]).reshape(block_len, top_count, row_width),
        axis=1,
    )
    return (h_res + moe_out).astype(jnp.bfloat16)[None]


def solution(mesh):
    in_specs = (
        P("exp", "seq", None),
        P("exp", "seq", None),
        P("exp", "seq", None),
        P("exp", "seq", None),
        P("exp", "seq", None),
        P(),
        P(),
        P("exp", "seq", None),
        P("exp", "seq", None),
        P("exp", None, None),
        P("exp", None, None),
        P("exp", None, None),
    )
    out_specs = P("exp", "seq", None)
    return jax.shard_map(
        per_device, mesh=mesh, in_specs=in_specs, out_specs=out_specs, check_vma=False
    )
```

profile of v0, /device:TPU:26, one launch (start us, length us, event | category | flops | bytes accessed | tf_op | source)
XLA Modules:
  0.0 303.7 jit_solution(8877984949286080626)
XLA Ops:
  6.5 0.9 copy_bitcast_fusion.1
  7.4 0.6 reduce-window.14
  8.0 0.2 slice_reduce_fusion.1
  8.3 0.2 slice_reduce_fusion.2
  8.5 2.3 copy.74
  10.8 1.5 copy.79
  12.3 1.0 copy-done.6
  13.3 3.5 %fusion.17 = bf16[16,128,128]{2,1,0:T(8,128)(2,1)} fusion(bf16[256,16,128]{0,2,1:T(8,128)(2,1)} %bitcast.114, f32[256,16]{0,1:T(8,128)S(1)} %get-tuple-element.61, bf16[256,16,128]{2,1,0:T(8,128)(2,1)S(1)} %bitcast.116), kind=kOutput, calls=%fused_computation.29 | convolution fusion | flops 806617088 | bytes 2637824 | tf_op jit(solution)/shard_map/thd,the->hde/dot_general | solution.py:66
  16.8 0.1 copy.67
  16.9 0.1 eq.29
  17.0 0.1 eq.25
  17.2 0.2 fusion.31
  17.4 7.3 %all-gather.1 = bf16[8,1,16]{2,1,0:T(2,128)(2,1)S(1)} all-gather(bf16[1,1,16]{2,1,0:T(2,128)(2,1)S(1)} %bitcast.122), channel_id=1, replica_groups=mesh['seq'=8,'exp'=32] {'seq'}, dimensions={0}, use_global_device_ids=true | all-gather | bytes 288 | tf_op jit(solution)/shard_map/all_gather | solution.py:10
  24.6 2.5 copy.78
  27.1 1.2 reduce-window.16
  28.3 0.2 slice_reduce_fusion
  28.6 0.1 copy.66
  28.7 0.1 mul.109
  29.0 5.1 %fusion.16 = f32[16,256,128]{1,2,0:T(8,128)} fusion(bf16[256,16,128]{0,2,1:T(8,128)(2,1)} %bitcast.115, f32[16,256]{1,0:T(8,128)S(1)} %get-tuple-element.63, pred[256,256]{1,0:T(8,128)(4,1)S(1)} %iota_compare_fusion, bf16[256,16,128]{2,1,0:T(8,128)(2,1)} %bitcast.117, bf16[256,16,128]{2,1,0:T(8,128)(2,1)} %bitcast.106), kind=kOutput, calls=%fused_computation.28 | convolution fusion | flops 542113792 | bytes 5324800 | tf_op jit(solution)/shard_map/hts,shd->thd/dot_general | solution.py:91
  34.1 18.3 %all-gather.4.cloned.1.call-done = bf16[128,128,128]{2,1,0:T(8,128)(2,1)} async-done(((bf16[16,128,128]{2,1,0:T(8,128)(2,1)}), bf16[128,128,128]{2,1,0:T(8,128)(2,1)}) %all-gather.4.cloned.1.call-update) | async-done | bytes 4194320 | tf_op jit(solution)/shard_map/all_gather | solution.py:10
  52.3 1.1 broadcast_in_dim.19
  53.4 15.1 %while.12 = (s32[]{:T(128)}, f32[16,128,128]{2,1,0:T(8,128)}, s32[]{:T(128)}, bf16[8,16]{1,0:T(8,128)(2,1)S(1)}, bf16[8,16,128,128]{3,2,1,0:T(8,128)(2,1)}, /*index=5*/s32[]{:T(128)}, s32[]{:T(128)}, s32[]{:T(128)}) while((s32[]{:T(128)}, f32[16,128,128]{2,1,0:T(8,128)}, s32[]{:T(128)}, bf16[8,16]{1,0:T(8,128)(2,1)S(1)}, ...), condition=%wide.region_3.4_spmd, body=%wide.region_2.3_spmd.sunk | while | flops 786453 | bytes 2621727 | solution.py:24
  53.4 2.5 convert_add_fusion.3
  55.9 2.5 convert_add_fusion.3
  58.5 2.5 convert_add_fusion.3
  61.0 2.5 convert_add_fusion.3
  63.5 2.5 convert_add_fusion.3
  66.0 2.5 convert_add_fusion.3
  68.5 3.6 %multiply_reduce_fusion.2 = (f32[256,16]{0,1:T(8,128)S(1)}, f32[256,16,128]{0,2,1:T(8,128)S(1)}) fusion(f32[16,128,128]{2,1,0:T(8,128)} %get-tuple-element.49, bf16[256,16,128]{2,1,0:T(8,128)(2,1)} %bitcast.107, f32[256,16]{0,1:T(8,128)S(1)} %get-tuple-element.60, f32[16,256,128]{1,2,0:T(8,128)} %fusion.16), kind=kOutput, calls=%fused_computation.22 | convolution fusion | flops 807399424 | bytes 6324224 | tf_op jit(solution)/shard_map/thd,hde->the/dot_general | solution.py:94
  72.1 1.6 broadcast_divide_fusion
  73.7 3.0 copy.70
  76.7 2.4 multiply_reduce_fusion.1
  79.2 0.3 copy-done.2
  79.5 0.4 divide_convert_fusion
  79.9 2.6 broadcast_in_dim.21
  82.6 4.1 %reshape.203 = bf16[512,2048]{1,0:T(8,128)(2,1)} reshape(bf16[256,2,2048]{2,1,0:T(2,128)(2,1)} %broadcast_in_dim.21) | data formatting | bytes 4194304 | tf_op jit(solution)/shard_map/reshape | solution.py:113
  86.7 6.7 %scatter_custom_fusion = bf16[768,2048]{1,0:T(8,128)(2,1)} fusion(s32[512]{0:T(512)S(1)} %bitcast.118, bf16[512,2048]{1,0:T(8,128)(2,1)} %reshape.203, bf16[]{:T(256)} %constant.53.clone.1), kind=kCustom, calls=%fused_computation.26 | custom fusion | bytes 3146240 | tf_op jit(solution)/shard_map/scatter | solution.py:114
  93.4 79.3 %all_to_all.10 = bf16[32,24,2048]{2,1,0:T(8,128)(2,1)S(1)} all-to-all(bf16[32,24,2048]{2,1,0:T(8,128)(2,1)} %bitcast.105), channel_id=1, replica_groups=mesh['seq'=8,'exp'=32] {'exp'}, dimensions={0} | all-to-all | bytes 6291456 | tf_op jit(solution)/shard_map/all_to_all | solution.py:117
  172.7 1.7 copy-done.5
  174.4 4.0 %fusion.1 = f32[768,768]{1,0:T(8,128)} fusion(bf16[768,2048]{1,0:T(8,128)(2,1)S(1)} %bitcast.109, bf16[1,2048,768]{2,1,0:T(8,128)(2,1)S(1)} %copy-done.11), kind=kOutput, calls=%fused_computation.8 | convolution fusion | flops 2415919104 | bytes 8650752 | tf_op jit(solution)/shard_map/dot_general | solution.py:31
  178.5 11.0 %convolution_convert_fusion = bf16[768,2048]{1,0:T(8,128)(2,1)} fusion(bf16[1,768,2048]{2,1,0:T(8,128)(2,1)S(1)} %copy-done, f32[768,768]{1,0:T(8,128)} %fusion.1, bf16[768,2048]{1,0:T(8,128)(2,1)} %bitcast.110, bf16[1,2048,768]{2,1,0:T(8,128)(2,1)} %param.23), kind=kOutput, calls=%fused_computation.6 | convolution fusion | flops 4836950016 | bytes 14942208 | tf_op jit(solution)/shard_map/dot_general | solution.py:33
  189.5 10.6 %all-to-all-start.1 = ((bf16[32,24,2048]{2,1,0:T(8,128)(2,1)}), bf16[32,24,2048]{2,1,0:T(8,128)(2,1)}, u32[]{:S(2)}, u32[]{:S(2)}) async-start(bf16[32,24,2048]{2,1,0:T(8,128)(2,1)} %bitcast.108), calls=%async_computation.1 | async-start | bytes 6291456 | tf_op jit(solution)/shard_map/all_to_all | solution.py:122
  200.2 2.9 copy.65
  203.1 70.2 %all-to-all-done.1 = bf16[32,24,2048]{2,1,0:T(8,128)(2,1)} async-done(((bf16[32,24,2048]{2,1,0:T(8,128)(2,1)}), bf16[32,24,2048]{2,1,0:T(8,128)(2,1)}, u32[]{:S(2)}, u32[]{:S(2)}) %all-to-all-start.1) | async-done | bytes 3145760 | tf_op jit(solution)/shard_map/all_to_all | solution.py:122
  273.3 7.5 %gather_fusion = bf16[512,2048]{1,0:T(8,128)(2,1)} fusion(bf16[768,2048]{1,0:T(8,128)(2,1)} %bitcast.20, s32[1024]{0:T(1024)S(1)} %pad_clamp_fusion), kind=kCustom, calls=%fused_computation | custom fusion | bytes 4196352 | tf_op jit(solution)/shard_map/gather | solution.py:123
  280.9 5.4 %reshape.190 = f32[256,2,2048]{2,1,0:T(2,128)} reshape(bf16[512,2048]{1,0:T(8,128)(2,1)} %gather_fusion) | data formatting | bytes 6291456 | tf_op jit(solution)/shard_map/convert_element_type | solution.py:126
  286.3 9.0 %multiply_reduce_fusion = f32[256,2048]{1,0:T(8,128)S(1)} fusion(f32[256,2,2048]{2,1,0:T(2,128)} %reshape.190, f32[256,2]{1,0:T(8,128)S(1)} %copy.71), kind=kLoop, calls=%fused_computation.4 | loop fusion | flops 1572864 | bytes 6293504 | tf_op jit(solution)/shard_map/reduce_sum | solution.py:125
  295.4 1.5 fusion.6
  (47 shorter events, 0.7 us)
Async XLA Ops:
  6.5 171.9 %copy-start = (bf16[1,768,2048]{2,1,0:T(8,128)(2,1)S(1)}, bf16[1,768,2048]{2,1,0:T(8,128)(2,1)}, u32[]{:S(2)}) copy-start(bf16[1,768,2048]{2,1,0:T(8,128)(2,1)} %param.25) | copy-start | bytes 9437188
  6.5 45.8 %all-gather.4.cloned.1.call-start = ((), (), s32[]{:S(2)}) async-start(), calls=%async_computation.2 | async-start | bytes 4718592 | tf_op jit(solution)/shard_map/all_gather | solution.py:10
  10.8 5.9 %copy-start.9 = (s32[1,256,2]{1,2,0:T(2,128)S(1)}, s32[1,256,2]{1,2,0:T(2,128)}, u32[]{:S(2)}) copy-start(s32[1,256,2]{1,2,0:T(2,128)} %param.21) | copy-start | bytes 6148
  12.3 1.0 copy-start.6
  73.7 3.0 copy-start.7
  76.7 2.5 copy-start.1
  76.7 2.8 copy-start.2
  76.7 2.8 copy-start.8
  93.4 81.0 %copy-start.11 = (bf16[1,2048,768]{2,1,0:T(8,128)(2,1)S(1)}, bf16[1,2048,768]{2,1,0:T(8,128)(2,1)}, u32[]{:S(2)}) copy-start(bf16[1,2048,768]{2,1,0:T(8,128)(2,1)} %param.24) | copy-start | bytes 9437188
  172.7 1.7 copy-start.5
  189.5 10.6 %copy-start.10 = (s32[1,256,2]{1,2,0:T(2,128)S(1)}, s32[1,256,2]{1,2,0:T(2,128)}, u32[]{:S(2)}) copy-start(s32[1,256,2]{1,2,0:T(2,128)} %param.22) | copy-start | bytes 6148
  189.5 83.9 %all-to-all-start.1 = ((bf16[32,24,2048]{2,1,0:T(8,128)(2,1)}), bf16[32,24,2048]{2,1,0:T(8,128)(2,1)}, u32[]{:S(2)}, u32[]{:S(2)}) async-start(bf16[32,24,2048]{2,1,0:T(8,128)(2,1)} %bitcast.108), calls=%async_computation.1 | async-start | bytes 6291456 | tf_op jit(solution)/shard_map/all_to_all | solution.py:122
  286.3 9.1 %copy-start.3 = (bf16[1,256,2048]{2,1,0:T(8,128)(2,1)S(1)}, bf16[1,256,2048]{2,1,0:T(8,128)(2,1)}, u32[]{:S(2)}) copy-start(bf16[1,256,2048]{2,1,0:T(8,128)(2,1)} %param.14) | copy-start | bytes 3145732
  286.3 9.1 %copy-start.4 = (f32[1,256,2048]{2,1,0:T(8,128)S(1)}, f32[1,256,2048]{2,1,0:T(8,128)}, u32[]{:S(2)}) copy-start(f32[1,256,2048]{2,1,0:T(8,128)} %copy.65) | copy-start | bytes 6291460
Sparse Core Ops, SparseCore 0:
  16.9 35.4 all-gather.3
where the time goes:
time: 305 us; the launch traced here: 304 us
  waiting for transfers between devices  88.5 us (29%)
  blocking collectives  86.6 us (28%)
  local copies, waits for them, and re-layouts  45.1 us (15%)
  other arithmetic  32.3 us (11%)
  matrix products  27.1 us (9%)
  between operations  13.6 us (4%)
  starting transfers between devices  10.6 us (3%)
    all_to_all x1, blocking collectives, per_device(): lax.all_to_all(send_rows, 'exp', split_axis=0, concat_axis=0, tiled=True)  79.3 us
    all_to_all x1, waiting for transfers between devices, per_device(): lax.all_to_all(expert_done, 'exp', split_axis=0, concat_axis=0, tiled=True)  70.2 us
    all_gather x1, waiting for transfers between devices, prefix(): lax.all_gather(a.astype(kind), axis)  18.3 us
    add x6, other arithmetic, combine(): jnp.exp(later_part[0])[:, None, None] * earlier[1] + later_part[1]  15 us
    dot_general x1, matrix products, expert_rows(): jnp.dot(activation, down_weight, preferred_element_type=jnp.float32)  11 us
    all_to_all x1, starting transfers between devices, per_device(): lax.all_to_all(expert_done, 'exp', split_axis=0, concat_axis=0, tiled=True)  10.6 us
    reduce_sum x1, other arithmetic, per_device(): jnp.sum((picked.astype(jnp.float32) * gate_scale[:, None]).reshape(block_...  9.04 us
    gather x1, local copies, waits for them, and re-layouts, per_device(): picked = returned.reshape(owners * capacity, row_width)[position]  7.52 us
  transfers between devices with their start and end apart: 2, of which 2 were waited for; matrix products, arithmetic and copies ran while one was open for 4% of the time, Pallas kernels for 0%

commit v1 on v0

v1 whole, which is shorter than its diff:
```python
import jax
import jax.numpy as jnp
from jax import lax
from jax.experimental import pallas as pl
from jax.experimental.pallas import tpu as pltpu
from jax.sharding import PartitionSpec as P

F32 = jnp.float32
BF16 = jnp.bfloat16
EXACT = lax.Precision.HIGHEST
VMEM_LIMIT = 56 * 1024 * 1024
LOG_ROWS = 16


def call(body, out_shape, **kw):
    return pl.pallas_call(
        body,
        out_shape=out_shape,
        compiler_params=pltpu.CompilerParams(vmem_limit_bytes=VMEM_LIMIT),
        **kw,
    )


def dot(a, b, ca=1, cb=0, precision=None):
    return lax.dot_general(
        a, b, (((ca,), (cb,)), ((), ())), precision=precision, preferred_element_type=F32
    )


def iota(shape, dim):
    return lax.broadcasted_iota(jnp.int32, shape, dim)


def contrib_body(k_ref, v_ref, decay_ref, out_ref, cum_ref, cum_t_ref):
    block, heads = decay_ref.shape
    groups = out_ref.shape[0]
    per = heads // groups
    dh = k_ref.shape[1] // heads
    lower = (iota((block, block), 0) >= iota((block, block), 1)).astype(F32)
    decay = decay_ref[...]
    cum = -dot(lower, decay, precision=EXACT)
    cum_t = -dot(decay, lower, 0, 1, precision=EXACT)
    cum_ref[...] = cum
    cum_t_ref[...] = cum_t
    total = cum[block - 1 : block, :]
    decayed = jnp.exp(total - cum)
    for g in range(groups):
        row = iota((LOG_ROWS, dh), 0)
        logs = jnp.zeros((LOG_ROWS, dh), F32)
        for i in range(per):
            h = g * per + i
            cols = slice(h * dh, (h + 1) * dh)
            kw = (k_ref[:, cols].astype(F32) * decayed[:, h : h + 1]).astype(BF16)
            out_ref[g, i * dh : (i + 1) * dh, :] = dot(kw, v_ref[:, cols], 0, 0).astype(BF16)
            rest = jnp.broadcast_to(total[:, h : h + 1], (LOG_ROWS, dh))
            for piece in range(3):
                part = rest.astype(BF16).astype(F32)
                logs = jnp.where(row == 3 * i + piece, part, logs)
                rest = rest - part
        out_ref[g, per * dh :, :] = logs.astype(BF16)


def prefix_body(x_ref, out_ref):
    blocks, rows, dh = out_ref.shape
    per = rows // dh
    for i in range(per):
        here = slice(i * dh, (i + 1) * dh)
        state = jnp.zeros((dh, dh), F32)
        for b in range(blocks):
            out_ref[b, here, :] = state.astype(BF16)
            pieces = [
                x_ref[b, rows + 3 * i + p : rows + 3 * i + p + 1, :].astype(F32) for p in range(3)
            ]
            state = jnp.exp(pieces[0] + pieces[1] + pieces[2]) * state + x_ref[b, here, :].astype(F32)


def intra_body(q_ref, k_ref, v_ref, cum_ref, cum_t_ref, out_ref):
    block, heads = cum_ref.shape
    dh = q_ref.shape[1] // heads
    half = block // 2
    cum = cum_ref[...]
    cum_t = cum_t_ref[...]
    for h in range(heads):
        cols = slice(h * dh, (h + 1) * dh)
        for lo, hi in ((0, half), (half, block)):
            scores = dot(q_ref[lo:hi, cols], k_ref[:hi, cols], 1, 1)
            gap = cum[lo:hi, h : h + 1] - cum_t[h : h + 1, :hi]
            seen = iota((hi - lo, hi), 0) + lo >= iota((hi - lo, hi), 1)
            probs = jnp.where(seen, scores * jnp.exp(jnp.minimum(gap, 0.0)), 0.0).astype(BF16)
            out_ref[lo:hi, cols] = dot(probs, v_ref[:hi, cols])


def finish_body(
    intra_ref, q_ref, carried_ref, cum_ref, x_ref, attn_gain_ref, norm_gain_ref, ids_ref, h_ref, send_ref, normed_ref
):
    block, heads = cum_ref.shape
    width = q_ref.shape[1]
    dh = width // heads
    per = carried_ref.shape[1] // dh
    grow = jnp.exp(cum_ref[...])
    squares = jnp.zeros((block, dh), F32)
    for h in range(heads):
        cols = slice(h * dh, (h + 1) * dh)
        state = carried_ref[h // per, (h % per) * dh : (h % per + 1) * dh, :]
        raw = intra_ref[:, cols] + grow[:, h : h + 1] * dot(q_ref[:, cols], state)
        scale = lax.rsqrt(jnp.mean(raw * raw, axis=-1, keepdims=True) + 1e-06)
        res = x_ref[:, cols].astype(F32) + attn_gain_ref[:, cols] * (raw * scale)
        h_ref[:, cols] = res
        squares = squares + res * res
    scale = lax.rsqrt(jnp.sum(squares, axis=-1, keepdims=True) / width + 1e-06)
    for h in range(heads):
        cols = slice(h * dh, (h + 1) * dh)
        normed_ref[:, cols] = (norm_gain_ref[:, cols] * h_ref[:, cols] * scale).astype(BF16)
    slots = send_ref.shape[0]
    experts = slots // (3 * block // 32)
    cap = slots // experts
    expert = iota((experts, block), 0)
    member = (ids_ref[0:1, :] == expert) | (ids_ref[1:2, :] == expert)
    member = member.astype(F32)
    earlier = (iota((block, block), 0) < iota((block, block), 1)).astype(BF16)
    rank = (dot(member.astype(BF16), earlier) + 1.0) * member
    spread = (iota((slots, experts), 0) // cap == iota((slots, experts), 1)).astype(BF16)
    ranks = dot(spread, rank.astype(BF16))
    wanted = (iota((slots, block), 0) % cap + 1).astype(F32)
    pick = (ranks == wanted).astype(BF16)
    step = 512
    for c in range(0, width, step):
        send_ref[:, c : c + step] = dot(pick, normed_ref[:, c : c + step]).astype(BF16)


def expert_body(x_ref, gate_ref, up_ref, down_ref, out_ref, act_ref, *, hidden_steps, hidden_block):
    i = pl.program_id(0)
    for j in range(hidden_steps):

        @pl.when(i == j)
        def _():
            x = x_ref[...]
            gate = dot(x, gate_ref[...])
            up = dot(x, up_ref[...])
            act_ref[:, j * hidden_block : (j + 1) * hidden_block] = (
                gate / (1.0 + jnp.exp(-gate)) * up
            ).astype(BF16)

    @pl.when(i >= hidden_steps)
    def _():
        out_ref[...] = dot(act_ref[...], down_ref[...]).astype(BF16)


def combine_body(back_ref, h_ref, ids_ref, levels_ref, out_ref, mix_ref):
    block = h_ref.shape[0]
    slots = back_ref.shape[0]

    @pl.when(pl.program_id(0) == 0)
    def _():
        experts = slots // (3 * block // 32)
        cap = slots // experts
        expert = iota((block, experts), 1)
        first = ids_ref[:, 0:1] == expert
        second = ids_ref[:, 1:2] == expert
        member = (first | second).astype(F32)
        later = (iota((block, block), 0) > iota((block, block), 1)).astype(BF16)
        rank = (dot(later, member.astype(BF16)) + 1.0) * member
        level = jnp.where(first, levels_ref[:, 0:1], 0) + jnp.where(second, levels_ref[:, 1:2], 0)
        spread = (iota((experts, slots), 1) // cap == iota((experts, slots), 0)).astype(BF16)
        ranks = dot(rank.astype(BF16), spread)
        levels = dot(level.astype(F32).astype(BF16), spread)
        wanted = (iota((block, slots), 1) % cap + 1).astype(F32)
        mix_ref[...] = jnp.where(ranks == wanted, levels * (1.0 / 256.0), 0.0).astype(BF16)

    out_ref[...] = (h_ref[...] + dot(mix_ref[...], back_ref[...])).astype(BF16)


def per_device(
    layer_input, queries, keys_in, values_in, decay_rate, attn_gain, norm_gain, expert_ids, gate_levels, w_gate, w_up, w_down
):
    x, q, k, v, decay = layer_input[0], queries[0], keys_in[0], values_in[0], decay_rate[0]
    ids, levels = expert_ids[0], gate_levels[0]
    gate, up, down = w_gate[0], w_up[0], w_down[0]
    block, width = x.shape
    heads = decay.shape[1]
    dh = width // heads
    groups = lax.axis_size("seq")
    experts = lax.axis_size("exp")
    cap = 3 * block // experts
    slots = experts * cap
    hidden = gate.shape[1]
    rows = heads // groups * dh

    states, cum, cum_t = call(
        contrib_body,
        (
            jax.ShapeDtypeStruct((groups, rows + LOG_ROWS, dh), BF16),
            jax.ShapeDtypeStruct((block, heads), F32),
            jax.ShapeDtypeStruct((heads, block), F32),
        ),
        name="contrib",
    )(k, v, decay)
    states = lax.all_to_all(states, "seq", 0, 0, tiled=True)
    carried = call(prefix_body, jax.ShapeDtypeStruct((groups, rows, dh), BF16), name="prefix")(states)
    carried = lax.all_to_all(carried, "seq", 0, 0, tiled=True)
    intra = call(intra_body, jax.ShapeDtypeStruct((block, width), F32), name="intra")(q, k, v, cum, cum_t)
    h_res, send = call(
        finish_body,
        (jax.ShapeDtypeStruct((block, width), F32), jax.ShapeDtypeStruct((slots, width), BF16)),
        scratch_shapes=[pltpu.VMEM((block, width), BF16)],
        name="finish",
    )(intra, q, carried, cum, x, attn_gain[None], norm_gain[None], ids.T)

    got = lax.all_to_all(send.reshape(experts, cap, width), "exp", 0, 0, tiled=True).reshape(slots, width)

    hidden_block = 256
    hidden_steps = hidden // hidden_block
    out_block = 512
    out_steps = width // out_block
    last = hidden_steps - 1
    done = call(
        lambda *refs: expert_body(*refs, hidden_steps=hidden_steps, hidden_block=hidden_block),
        jax.ShapeDtypeStruct((slots, width), BF16),
        grid=(hidden_steps + out_steps,),
        in_specs=[
            pl.BlockSpec((slots, width), lambda i: (0, 0)),
            pl.BlockSpec((width, hidden_block), lambda i: (0, jnp.minimum(i, last))),
            pl.BlockSpec((width, hidden_block), lambda i: (0, jnp.minimum(i, last))),
            pl.BlockSpec((hidden, out_block), lambda i: (0, jnp.maximum(i - hidden_steps, 0))),
        ],
        out_specs=pl.BlockSpec((slots, out_block), lambda i: (0, jnp.maximum(i - hidden_steps, 0))),
        scratch_shapes=[pltpu.VMEM((slots, hidden), BF16)],
        name="expert",
    )(got, gate, up, down)

    back = lax.all_to_all(done.reshape(experts, cap, width), "exp", 0, 0, tiled=True).reshape(slots, width)

    out = call(
        combine_body,
        jax.ShapeDtypeStruct((block, width), BF16),
        grid=(width // out_block,),
        in_specs=[
            pl.BlockSpec((slots, out_block), lambda i: (0, i)),
            pl.BlockSpec((block, out_block), lambda i: (0, i)),
            pl.BlockSpec(ids.shape, lambda i: (0, 0)),
            pl.BlockSpec(levels.shape, lambda i: (0, 0)),
        ],
        out_specs=pl.BlockSpec((block, out_block), lambda i: (0, i)),
        scratch_shapes=[pltpu.VMEM((block, slots), BF16)],
        name="combine",
    )(back, h_res, ids, levels)
    return out[None]


def solution(mesh):
    tokens = P("exp", "seq", None)
    whole = P()
    weights = P("exp", None, None)
    return jax.shard_map(
        per_device,
        mesh=mesh,
        in_specs=(tokens,) * 5 + (whole,) * 2 + (tokens,) * 2 + (weights,) * 3,
        out_specs=tokens,
        check_vma=False,
    )
```

time: 305 us -> 230 us (0.75)
  the two profiles are of different devices: /device:TPU:26 before, /device:TPU:32 now
where the time goes in v1:
time: 230 us; the launch traced here: 226 us
  blocking collectives  99.9 us (43%)
  waiting for transfers between devices  71.7 us (31%)
  Pallas kernels  39.6 us (17%)
  starting transfers between devices  8.81 us (4%)
  local copies, waits for them, and re-layouts  5.5 us (2%)
    all_to_all x1, blocking collectives, per_device(): lax.all_to_all(send.reshape(experts, cap, width), 'exp', 0, 0, tiled=True)  84.6 us
    all_to_all x1, waiting for transfers between devices, per_device(): lax.all_to_all(done.reshape(experts, cap, width), 'exp', 0, 0, tiled=True)  68.8 us
    all_to_all x1, blocking collectives, per_device(): states = lax.all_to_all(states, 'seq', 0, 0, tiled=True)  15.3 us
    pallas_call x1, Pallas kernels, per_device(): call(lambda *refs: expert_body(*refs, hidden_steps=hidden_steps, hidden_b...  13.8 us
    pallas_call x1, Pallas kernels, per_device(): call(finish_body, (jax.ShapeDtypeStruct((block, width), F32), jax.ShapeDt...  7.27 us
    pallas_call x1, Pallas kernels, per_device(): call(intra_body, jax.ShapeDtypeStruct((block, width), F32), name='intra')  6.58 us
    pallas_call x1, Pallas kernels, per_device(): call(combine_body, jax.ShapeDtypeStruct((block, width), BF16), grid=(widt...  5.63 us
    all_to_all x1, starting transfers between devices, per_device(): lax.all_to_all(done.reshape(experts, cap, width), 'exp', 0, 0, tiled=True)  5.32 us
  transfers between devices with their start and end apart: 2, of which 2 were waited for; matrix products, arithmetic and copies ran while one was open for 1% of the time, Pallas kernels for 3%

profile of v1, /device:TPU:32, one launch (start us, length us, event | category | flops | bytes accessed | tf_op | source)
XLA Modules:
  0.0 225.6 jit_solution(17107056120887048473)
XLA Ops:
  0.0 0.0 copy-start.3
  0.0 1.5 copy.13
  1.5 4.3 %contrib.1 = (bf16[8,272,128]{2,1,0:T(8,128)(2,1)}, f32[256,16]{1,0:T(8,128)}, f32[16,256]{1,0:T(8,128)}) custom-call(bf16[256,2048]{1,0:T(8,128)(2,1)} %bitcast.22, bf16[256,2048]{1,0:T(8,128)(2,1)} %bitcast.24, f32[256,16]{1,0:T(8,128)} %bitcast.36), custom_call_target="tpu_custom_call" | custom-call | tf_op jit(solution)/shard_map/contrib/pallas_call | solution.py:189
  5.8 15.3 %all_to_all.20.x_ref = bf16[8,272,128]{2,1,0:T(8,128)(2,1)} all-to-all(bf16[8,272,128]{2,1,0:T(8,128)(2,1)} %get-tuple-element.12), channel_id=1, replica_groups=mesh['seq'=8,'exp'=32] {'seq'}, dimensions={0} | all-to-all | bytes 1114112 | tf_op jit(solution)/shard_map/all_to_all | solution.py:198
  21.1 2.0 prefix.1
  23.1 3.5 %all-to-all-start.1 = ((bf16[8,256,128]{2,1,0:T(8,128)(2,1)}), bf16[8,256,128]{2,1,0:T(8,128)(2,1)S(1)}, u32[]{:S(2)}, u32[]{:S(2)}) async-start(bf16[8,256,128]{2,1,0:T(8,128)(2,1)} %prefix.1), calls=%async_computation.1 | async-start | bytes 1048576 | tf_op jit(solution)/shard_map/all_to_all | solution.py:200
  26.6 0.0 copy-done.3
  26.6 0.1 copy.14
  26.7 0.0 copy-start.2
  26.7 0.7 copy.15.ids_ref
  27.4 6.6 %intra.1.intra_ref = f32[256,2048]{1,0:T(8,128)} custom-call(bf16[256,2048]{1,0:T(8,128)(2,1)} %bitcast.26, bf16[256,2048]{1,0:T(8,128)(2,1)} %bitcast.23, bf16[256,2048]{1,0:T(8,128)(2,1)} %bitcast.25, f32[256,16]{1,0:T(8,128)} %get-tuple-element.10.cum_ref, f32[16,256]{1,0:T(8,128)} %get-tuple-element.11.cum_t_ref), custom_call_target="tpu_custom_call" | custom-call | tf_op jit(solution)/shard_map/intra/pallas_call | solution.py:201
  34.0 2.9 %all-to-all-done.1.carried_ref = bf16[8,256,128]{2,1,0:T(8,128)(2,1)S(1)} async-done(((bf16[8,256,128]{2,1,0:T(8,128)(2,1)}), bf16[8,256,128]{2,1,0:T(8,128)(2,1)S(1)}, u32[]{:S(2)}, u32[]{:S(2)}) %all-to-all-start.1) | async-done | bytes 524320 | tf_op jit(solution)/shard_map/all_to_all | solution.py:200
  36.8 0.0 copy-start.1
  36.8 0.8 copy-done.1
  37.6 7.3 %finish.1 = (f32[256,2048]{1,0:T(8,128)}, bf16[768,2048]{1,0:T(8,128)(2,1)}) custom-call(f32[256,2048]{1,0:T(8,128)} %intra.1.intra_ref, bf16[256,2048]{1,0:T(8,128)(2,1)} %bitcast.27, bf16[8,256,128]{2,1,0:T(8,128)(2,1)} %copy-done.1, f32[256,16]{1,0:T(8,128)} %get-tuple-element.10.cum_ref, bf16[256,2048]{1,0:T(8,128)(2,1)} %bitcast.34, ...), custom_call_target="tpu_custom_call" | custom-call | tf_op jit(solution)/shard_map/finish/pallas_call | solution.py:202
  44.9 0.0 copy-done.2
  44.9 84.6 %all_to_all.21 = bf16[32,24,2048]{2,1,0:T(8,128)(2,1)} all-to-all(bf16[32,24,2048]{2,1,0:T(8,128)(2,1)} %bitcast.28), channel_id=1, replica_groups=mesh['seq'=8,'exp'=32] {'exp'}, dimensions={0} | all-to-all | bytes 6291456 | tf_op jit(solution)/shard_map/all_to_all | solution.py:209
  129.5 13.8 %expert.1 = bf16[768,2048]{1,0:T(8,128)(2,1)} custom-call(bf16[768,2048]{1,0:T(8,128)(2,1)} %bitcast.21, bf16[2048,768]{1,0:T(8,128)(2,1)} %bitcast.29, bf16[2048,768]{1,0:T(8,128)(2,1)} %bitcast.30, bf16[768,2048]{1,0:T(8,128)(2,1)} %bitcast.31), custom_call_target="tpu_custom_call" | custom-call | tf_op jit(solution)/shard_map/expert/pallas_call | solution.py:216
  143.3 0.0 copy-start.4
  143.3 5.3 %all-to-all-start.3 = ((bf16[32,24,2048]{2,1,0:T(8,128)(2,1)}), bf16[32,24,2048]{2,1,0:T(8,128)(2,1)S(1)}, u32[]{:S(2)}, u32[]{:S(2)}) async-start(bf16[32,24,2048]{2,1,0:T(8,128)(2,1)} %bitcast.20), calls=%async_computation.3 | async-start | bytes 6291456 | tf_op jit(solution)/shard_map/all_to_all | solution.py:231
  148.6 0.0 copy-done.4
  148.6 0.8 copy.16
  149.4 68.8 %all-to-all-done.3 = bf16[32,24,2048]{2,1,0:T(8,128)(2,1)S(1)} async-done(((bf16[32,24,2048]{2,1,0:T(8,128)(2,1)}), bf16[32,24,2048]{2,1,0:T(8,128)(2,1)S(1)}, u32[]{:S(2)}, u32[]{:S(2)}) %all-to-all-start.3) | async-done | bytes 3145760 | tf_op jit(solution)/shard_map/all_to_all | solution.py:231
  218.3 0.0 copy-start
  218.3 1.6 copy-done
  219.9 5.6 %combine.1 = bf16[256,2048]{1,0:T(8,128)(2,1)} custom-call(bf16[768,2048]{1,0:T(8,128)(2,1)} %bitcast.19, f32[256,2048]{1,0:T(8,128)} %get-tuple-element.14.h_ref, s32[256,2]{1,0:T(8,128)} %bitcast.33, s32[256,2]{1,0:T(8,128)} %bitcast.35), custom_call_target="tpu_custom_call" | custom-call | tf_op jit(solution)/shard_map/combine/pallas_call | solution.py:233
Async XLA Ops:
  0.0 26.6 %copy-start.3 = (s32[1,256,2]{1,2,0:T(2,128)S(1)}, s32[1,256,2]{1,2,0:T(2,128)}, u32[]{:S(2)}) copy-start(s32[1,256,2]{1,2,0:T(2,128)} %param.19) | copy-start | bytes 6148
  23.1 13.8 %all-to-all-start.1 = ((bf16[8,256,128]{2,1,0:T(8,128)(2,1)}), bf16[8,256,128]{2,1,0:T(8,128)(2,1)S(1)}, u32[]{:S(2)}, u32[]{:S(2)}) async-start(bf16[8,256,128]{2,1,0:T(8,128)(2,1)} %prefix.1), calls=%async_computation.1 | async-start | bytes 1048576 | tf_op jit(solution)/shard_map/all_to_all | solution.py:200
  26.7 18.2 %copy-start.2 = (s32[1,256,2]{2,1,0:T(8,128)}, s32[1,256,2]{2,1,0:T(8,128)S(1)}, u32[]{:S(2)}) copy-start(s32[1,256,2]{2,1,0:T(8,128)S(1)} %copy.14) | copy-start | bytes 6148
  36.8 0.8 copy-start.1
  143.3 5.3 %copy-start.4 = (s32[1,256,2]{1,2,0:T(2,128)S(1)}, s32[1,256,2]{1,2,0:T(2,128)}, u32[]{:S(2)}) copy-start(s32[1,256,2]{1,2,0:T(2,128)} %param.20) | copy-start | bytes 6148
  143.3 75.0 %all-to-all-start.3 = ((bf16[32,24,2048]{2,1,0:T(8,128)(2,1)}), bf16[32,24,2048]{2,1,0:T(8,128)(2,1)S(1)}, u32[]{:S(2)}, u32[]{:S(2)}) async-start(bf16[32,24,2048]{2,1,0:T(8,128)(2,1)} %bitcast.20), calls=%async_computation.3 | async-start | bytes 6291456 | tf_op jit(solution)/shard_map/all_to_all | solution.py:231
  218.3 1.6 copy-start

commit v2 on v1

v2 whole, which is shorter than its diff:
```python
import jax
import jax.numpy as jnp
from jax import lax
from jax.experimental import pallas as pl
from jax.experimental.pallas import tpu as pltpu
from jax.sharding import PartitionSpec as P

F32 = jnp.float32
BF16 = jnp.bfloat16
EXACT = lax.Precision.HIGHEST
VMEM_LIMIT = 24 * 1024 * 1024
PIECES = 3
LOG_ROWS = 32

VMEM_SPEC = pl.BlockSpec(memory_space=pltpu.VMEM)
SMEM_SPEC = pl.BlockSpec(memory_space=pltpu.SMEM)


def near(x):
    return pltpu.with_memory_space_constraint(x, pltpu.VMEM)


def local(body, name, outs, *args, scalars=None, scratch=()):
    specs = [VMEM_SPEC] * len(args)
    given = [near(a) for a in args]
    if scalars is not None:
        specs, given = [SMEM_SPEC, *specs], [scalars, *given]
    made = pl.pallas_call(
        body,
        out_shape=tuple(pltpu.VMEM(shape, dtype) for shape, dtype in outs),
        in_specs=specs,
        out_specs=tuple(VMEM_SPEC for _ in outs),
        scratch_shapes=list(scratch),
        compiler_params=pltpu.CompilerParams(vmem_limit_bytes=VMEM_LIMIT),
        name=name,
    )(*given)
    return made[0] if len(outs) == 1 else made


def dot(a, b, ca=1, cb=0, precision=None):
    return lax.dot_general(
        a, b, (((ca,), (cb,)), ((), ())), precision=precision, preferred_element_type=F32
    )


def iota(shape, dim):
    return lax.broadcasted_iota(jnp.int32, shape, dim)


def log_rows(logs, dh):
    row = iota((LOG_ROWS, dh), 0)
    out = jnp.zeros((LOG_ROWS, dh), F32)
    for i, rest in enumerate(logs):
        for piece in range(PIECES):
            part = rest.astype(BF16).astype(F32)
            out = jnp.where(row == PIECES * i + piece, part, out)
            rest = rest - part
    return out.astype(BF16)


def log_of(ref, i):
    first = ref.shape[0] - LOG_ROWS + PIECES * i
    a, b, c = (ref[first + p : first + p + 1, :].astype(F32) for p in range(PIECES))
    return a + b + c


def contrib_body(half_ref, k_ref, v_ref, decay_ref, out_ref):
    heads, block = decay_ref.shape
    dh = k_ref.shape[1] // heads
    lower = (iota((block, block), 0) >= iota((block, block), 1)).astype(F32)
    cum = -dot(lower, decay_ref[...], 1, 1, precision=EXACT)
    total = cum[block - 1 : block, :]
    decayed = jnp.exp(total - cum)
    logs = []
    for h in range(heads):
        cols = slice(h * dh, (h + 1) * dh)
        kw = (k_ref[:, cols].astype(F32) * decayed[:, h : h + 1]).astype(BF16)
        out_ref[cols, :] = dot(kw, v_ref[:, cols], 0, 0).astype(BF16)
        logs.append(jnp.broadcast_to(total[:, h : h + 1], (1, dh)))
    out_ref[heads * dh :, :] = log_rows(logs, dh)


def pair_body(place_ref, own_ref, other_ref, out_ref):
    dh = own_ref.shape[1]
    heads = (own_ref.shape[0] - LOG_ROWS) // dh
    is_even = place_ref[0] == 0
    logs = []
    for h in range(heads):
        rows = slice(h * dh, (h + 1) * dh)
        own, other = own_ref[rows, :].astype(F32), other_ref[rows, :].astype(F32)
        own_log, other_log = log_of(own_ref, h), log_of(other_ref, h)
        even, odd = jnp.where(is_even, own, other), jnp.where(is_even, other, own)
        out_ref[rows, :] = (jnp.exp(jnp.where(is_even, other_log, own_log)) * even + odd).astype(BF16)
        logs.append(own_log + other_log)
    out_ref[heads * dh :, :] = log_rows(logs, dh)


def carry_body(place_ref, own_ref, other_ref, *refs):
    *earlier, keep_ref, send_ref = refs
    dh = own_ref.shape[1]
    heads = keep_ref.shape[0] // dh
    is_even = place_ref[0] == 0
    chip = place_ref[1]
    for h in range(heads):
        rows = slice(h * dh, (h + 1) * dh)
        state = jnp.zeros((dh, dh), F32)
        for back in range(len(earlier), 0, -1):
            ref = earlier[back - 1]
            joined = jnp.exp(log_of(ref, h)) * state + ref[rows, :].astype(F32)
            state = jnp.where(chip >= back, joined, 0.0)
        even = jnp.where(is_even, own_ref[rows, :].astype(F32), other_ref[rows, :].astype(F32))
        even_log = jnp.where(is_even, log_of(own_ref, h), log_of(other_ref, h))
        after = jnp.exp(even_log) * state + even
        keep_ref[rows, :] = jnp.where(is_even, state, after).astype(BF16)
        send_ref[rows, :] = jnp.where(is_even, after, state).astype(BF16)


def intra_body(q_ref, k_ref, v_ref, decay_ref, out_ref, grow_ref):
    heads, block = decay_ref.shape
    dh = q_ref.shape[1] // heads
    half = block // 2
    lower = (iota((block, block), 0) >= iota((block, block), 1)).astype(F32)
    decay = decay_ref[...]
    cum = -dot(lower, decay, 1, 1, precision=EXACT)
    cum_t = -dot(decay, lower, 1, 1, precision=EXACT)
    grow_ref[...] = jnp.exp(cum)
    for h in range(heads):
        cols = slice(h * dh, (h + 1) * dh)
        for lo, hi in ((0, half), (half, block)):
            scores = dot(q_ref[lo:hi, cols], k_ref[:hi, cols], 1, 1)
            gap = cum[lo:hi, h : h + 1] - cum_t[h : h + 1, :hi]
            seen = iota((hi - lo, hi), 0) + lo >= iota((hi - lo, hi), 1)
            probs = jnp.where(seen, scores * jnp.exp(jnp.minimum(gap, 0.0)), 0.0).astype(BF16)
            out_ref[lo:hi, cols] = dot(probs, v_ref[:hi, cols])


def route_body(ids_ref, levels_ref, pick_ref, mix_ref, *, cap):
    slots, block = pick_ref.shape
    experts = slots // cap
    expert = iota((experts, block), 0)
    first = ids_ref[0:1, :] == expert
    second = ids_ref[1:2, :] == expert
    member = (first | second).astype(F32)
    earlier = (iota((block, block), 0) < iota((block, block), 1)).astype(BF16)
    rank = ((dot(member.astype(BF16), earlier) + 1.0) * member).astype(BF16)
    level = jnp.where(first, levels_ref[0:1, :], 0) + jnp.where(second, levels_ref[1:2, :], 0)
    level = level.astype(F32).astype(BF16)
    spread = (iota((slots, experts), 0) // cap == iota((slots, experts), 1)).astype(BF16)
    pick_ref[...] = (dot(spread, rank) == (iota((slots, block), 0) % cap + 1).astype(F32)).astype(BF16)
    spread = (iota((experts, slots), 1) // cap == iota((experts, slots), 0)).astype(BF16)
    used = dot(rank, spread, 0, 0) == (iota((block, slots), 1) % cap + 1).astype(F32)
    mix_ref[...] = jnp.where(used, dot(level, spread, 0, 0) * (1.0 / 256.0), 0.0).astype(BF16)


def finish_body(
    place_ref, intra_ref, q_ref, keep_ref, got_ref, grow_ref, x_ref, attn_gain_ref, norm_gain_ref, pick_ref, h_ref, send_ref
):
    block, heads = grow_ref.shape
    width = q_ref.shape[1]
    dh = width // heads
    per = heads // 2
    core = place_ref[0]
    squares = jnp.zeros((block, dh), F32)
    for h in range(heads):
        cols = slice(h * dh, (h + 1) * dh)
        rows = slice(h % per * dh, (h % per + 1) * dh)
        state = jnp.where(core == h // per, keep_ref[rows, :].astype(F32), got_ref[rows, :].astype(F32))
        raw = intra_ref[:, cols] + grow_ref[:, h : h + 1] * dot(q_ref[:, cols], state.astype(BF16))
        scale = lax.rsqrt(jnp.mean(raw * raw, axis=-1, keepdims=True) + 1e-06)
        res = x_ref[:, cols].astype(F32) + attn_gain_ref[:, cols] * (raw * scale)
        h_ref[:, cols] = res
        squares = squares + res * res
    scale = lax.rsqrt(jnp.sum(squares, axis=-1, keepdims=True) / width + 1e-06)
    step = 512
    for c in range(0, width, step):
        cols = slice(c, c + step)
        normed = (norm_gain_ref[:, cols] * h_ref[:, cols] * scale).astype(BF16)
        send_ref[:, cols] = dot(pick_ref[...], normed).astype(BF16)


def expert_body(x_ref, gate_ref, up_ref, down_ref, out_ref, act_ref):
    hidden, width = down_ref.shape
    step = 256
    for c in range(0, hidden, step):
        cols = slice(c, c + step)
        gate = dot(x_ref[...], gate_ref[:, cols])
        up = dot(x_ref[...], up_ref[:, cols])
        act_ref[:, cols] = (gate / (1.0 + jnp.exp(-gate)) * up).astype(BF16)
    for c in range(0, width, step):
        cols = slice(c, c + step)
        out_ref[:, cols] = dot(act_ref[...], down_ref[:, cols]).astype(BF16)


def combine_body(back_ref, h_ref, mix_ref, out_ref):
    step = 512
    for c in range(0, h_ref.shape[1], step):
        cols = slice(c, c + step)
        out_ref[:, cols] = (h_ref[:, cols] + dot(mix_ref[...], back_ref[:, cols])).astype(BF16)


def contribution(half, k, v, decay_t):
    heads, block = decay_t.shape
    width = k.shape[1]
    dh = width // heads
    return pl.pallas_call(
        contrib_body,
        out_shape=pltpu.VMEM((width // 2 + LOG_ROWS, dh), BF16),
        grid_spec=pltpu.PrefetchScalarGridSpec(
            num_scalar_prefetch=1,
            grid=(1,),
            in_specs=[
                pl.BlockSpec((block, width // 2), lambda i, half: (0, half[0])),
                pl.BlockSpec((block, width // 2), lambda i, half: (0, half[0])),
                pl.BlockSpec((heads // 2, block), lambda i, half: (half[0], 0)),
            ],
            out_specs=VMEM_SPEC,
        ),
        compiler_params=pltpu.CompilerParams(vmem_limit_bytes=VMEM_LIMIT),
        name="contrib",
    )(half, k, v, decay_t)


def carried_states(k, v, decay_t, place):
    blocks = lax.axis_size("seq")
    chips = blocks // 2
    dh = k.shape[1] // decay_t.shape[0]
    core = place[:1]
    swap = [(i, i ^ 1) for i in range(blocks)]

    def along(by):
        return [(i, (i // 2 + by) % chips * 2 + i % 2) for i in range(blocks)]

    other = lax.ppermute(contribution(1 - core, k, v, decay_t), "seq", swap)
    own = contribution(core, k, v, decay_t)
    pair = local(pair_body, "pair", [(own.shape, BF16)], own, other, scalars=place)
    earlier = [lax.ppermute(pair, "seq", along(by)) for by in range(1, chips)]
    half = ((own.shape[0] - LOG_ROWS, dh), BF16)
    keep, send = local(carry_body, "carry", [half, half], own, other, *earlier, scalars=place)
    return keep, lax.ppermute(send, "seq", swap)


def per_device(
    layer_input, queries, keys_in, values_in, decay_rate, attn_gain, norm_gain, expert_ids, gate_levels, w_gate, w_up, w_down
):
    x, q, k, v, decay_t = layer_input[0], queries[0], keys_in[0], values_in[0], decay_rate[0].T
    block, width = x.shape
    heads = decay_t.shape[0]
    experts = lax.axis_size("exp")
    cap = 3 * block // experts
    slots = experts * cap
    hidden = w_gate.shape[2]
    index = lax.axis_index("seq")
    place = jnp.stack([index % 2, index // 2]).astype(jnp.int32)

    keep, got = carried_states(k, v, decay_t, place)
    intra, grow = local(
        intra_body, "intra", [((block, width), F32), ((block, heads), F32)], q, k, v, decay_t
    )
    pick, mix = local(
        lambda *refs: route_body(*refs, cap=cap),
        "route",
        [((slots, block), BF16), ((block, slots), BF16)],
        expert_ids[0].T,
        gate_levels[0].T,
    )
    h_res, send = local(
        finish_body,
        "finish",
        [((block, width), F32), ((slots, width), BF16)],
        *(intra, q, keep, got, grow, x, attn_gain[None], norm_gain[None], pick),
        scalars=place,
    )
    arrived = lax.all_to_all(send.reshape(experts, cap, width), "exp", 0, 0, tiled=True)
    done = local(
        expert_body,
        "expert",
        [((slots, width), BF16)],
        *(arrived.reshape(slots, width), w_gate[0], w_up[0], w_down[0]),
        scratch=[pltpu.VMEM((slots, hidden), BF16)],
    )
    back = lax.all_to_all(done.reshape(experts, cap, width), "exp", 0, 0, tiled=True)
    out = local(
        combine_body, "combine", [((block, width), BF16)], back.reshape(slots, width), h_res, mix
    )
    return out[None]


def solution(mesh):
    tokens = P("exp", "seq", None)
    whole = P()
    weights = P("exp", None, None)
    return jax.shard_map(
        per_device,
        mesh=mesh,
        in_specs=(tokens,) * 5 + (whole,) * 2 + (tokens,) * 2 + (weights,) * 3,
        out_specs=tokens,
        check_vma=False,
    )
```

time: 230 us -> 213 us (0.926); the launches traced: 226 us -> 213 us
  blocking collectives: 99.9 us -> 164 us
  waiting for transfers between devices: 71.7 us -> 14.3 us
  Pallas kernels: 39.6 us -> 22 us
  starting transfers between devices: 8.81 us -> 4.98 us
    all_to_all x2 -> x0, waiting for transfers between devices: 71.7 us -> none  [the longest x1 68.8 us: per_device(): lax.all_to_all(done.reshape(experts, cap, width), 'exp', 0, 0, tiled=True)]
    all_to_all x1, blocking collectives: 15.3 us -> 78.6 us  [per_device(): lax.all_to_all(done.reshape(experts, cap, width), 'exp', 0, 0, tiled=True)]
    pallas_call x6 -> x9, Pallas kernels: 39.6 us -> 22 us  [the longest x7 18.9 us: local(): pl.pallas_call(body, out_shape=tuple((pltpu.VMEM(shape, dtype) for shape,...]
    ppermute x0 -> x5, waiting for transfers between devices: none -> 14.3 us  [the longest x3 14.3 us: carried_states(): earlier = [lax.ppermute(pair, 'seq', along(by)) for by in range(1, chips)]]
    all_to_all x2 -> x0, starting transfers between devices: 8.81 us -> none  [the longest x1 5.32 us: per_device(): lax.all_to_all(done.reshape(experts, cap, width), 'exp', 0, 0, tiled=True)]
    ppermute x0 -> x5, starting transfers between devices: none -> 4.98 us  [the longest x3 4.69 us: carried_states(): earlier = [lax.ppermute(pair, 'seq', along(by)) for by in range(1, chips)]]
    unnamed x13 -> x37, local copies, waits for them, and re-layouts: 4.84 us -> 7.37 us
  transfers between devices with their start and end apart: 2 -> 5, of which waited for: 2 -> 2; matrix products, arithmetic and copies ran while one was open for 1% -> 0% of each run, Pallas kernels for 3% -> 3%
where the time goes in v2:
time: 213 us
  blocking collectives  164 us (77%)
  Pallas kernels  22 us (10%)
  waiting for transfers between devices  14.3 us (7%)
  local copies, waits for them, and re-layouts  7.37 us (3%)
  starting transfers between devices  4.98 us (2%)
    all_to_all x1, blocking collectives, per_device(): lax.all_to_all(send.reshape(experts, cap, width), 'exp', 0, 0, tiled=True)  84.9 us
    all_to_all x1, blocking collectives, per_device(): lax.all_to_all(done.reshape(experts, cap, width), 'exp', 0, 0, tiled=True)  78.6 us
    pallas_call x7, Pallas kernels, local(): pl.pallas_call(body, out_shape=tuple((pltpu.VMEM(shape, dtype) for shape,...  18.9 us
    ppermute x3, waiting for transfers between devices, carried_states(): earlier = [lax.ppermute(pair, 'seq', along(by)) for by in range(1, chips)]  14.3 us
    unnamed x37, local copies, waits for them, and re-layouts  7.37 us
    ppermute x3, starting transfers between devices, carried_states(): earlier = [lax.ppermute(pair, 'seq', along(by)) for by in range(1, chips)]  4.69 us
  transfers between devices with their start and end apart: 5, of which 2 were waited for; matrix products, arithmetic and copies ran while one was open for 0% of the time, Pallas kernels for 3%

profile of v2, /device:TPU:32, one launch (start us, length us, event | category | flops | bytes accessed | tf_op | source)
XLA Modules:
  0.0 212.5 jit_solution(17510287823346608526)
XLA Ops:
  0.0 1.2 copy-done
  1.2 1.2 copy-done.3
  2.5 0.7 copy-done.11
  3.2 1.9 contrib.3
  5.1 0.0 collective-permute-start
  5.1 1.2 copy-done.1
  6.4 1.2 copy-done.4
  7.6 0.7 copy-done.12
  8.3 1.2 contrib.2.own_ref
  9.5 0.0 copy-start.16
  9.5 0.0 copy-start.17
  9.6 0.0 copy-start.14
  9.6 0.0 copy-start.15
  9.6 0.0 copy-start.10
  9.6 0.1 pad_add_fusion.place_ref
  9.7 0.0 collective-permute-done.other_ref
  9.7 1.2 pair.1
  10.9 3.1 %collective-permute-start.3 = (bf16[1056,128]{1,0:T(8,128)(2,1)S(1)}, bf16[1056,128]{1,0:T(8,128)(2,1)S(1)}, u32[]{:S(2)}, u32[]{:S(2)}) collective-permute-start(bf16[1056,128]{1,0:T(8,128)(2,1)S(1)} %pair.1), channel_id=1, source_target_pairs={{0,192},{32,224},{64,0},{96,32},{128,64},{160,96},{192,128},{224,1... | collective-permute-start | bytes 811016 | tf_op jit(solution)/shard_map/ppermute | solution.py:236
  14.0 0.6 collective-permute-start.2
  14.6 1.0 collective-permute-start.1
  15.6 10.6 %collective-permute-done.3.refs_2_ = bf16[1056,128]{1,0:T(8,128)(2,1)S(1)} collective-permute-done((bf16[1056,128]{1,0:T(8,128)(2,1)S(1)}, bf16[1056,128]{1,0:T(8,128)(2,1)S(1)}, u32[]{:S(2)}, u32[]{:S(2)}) %collective-permute-start.3) | collective-permute-done | bytes 270368 | tf_op jit(solution)/shard_map/ppermute | solution.py:236
  26.2 0.0 collective-permute-done.2.refs_1_
  26.2 3.7 %collective-permute-done.1.refs_0_ = bf16[1056,128]{1,0:T(8,128)(2,1)S(1)} collective-permute-done((bf16[1056,128]{1,0:T(8,128)(2,1)S(1)}, bf16[1056,128]{1,0:T(8,128)(2,1)S(1)}, u32[]{:S(2)}, u32[]{:S(2)}) %collective-permute-start.1) | collective-permute-done | bytes 270368 | tf_op jit(solution)/shard_map/ppermute | solution.py:236
  29.9 1.3 carry.1
  31.2 0.3 collective-permute-start.4
  31.5 0.0 copy-done.2
  31.5 0.0 copy-done.5
  31.5 0.0 copy-done.13
  31.5 0.0 copy-done.6
  31.6 3.6 %intra.1 = (f32[256,2048]{1,0:T(8,128)S(1)}, f32[256,16]{1,0:T(8,128)S(1)}) custom-call(bf16[256,2048]{1,0:T(8,128)(2,1)S(1)} %bitcast.35, bf16[256,2048]{1,0:T(8,128)(2,1)S(1)} %bitcast.31, bf16[256,2048]{1,0:T(8,128)(2,1)S(1)} %bitcast.34, f32[16,256]{1,0:T(8,128)S(1)} %bitcast.44), custom_call_target="tpu_custom_call" | custom-call | tf_op jit(solution)/shard_map/intra/pallas_call | solution.py:28
  35.2 0.0 copy-done.16
  35.2 0.0 copy-done.17
  35.2 0.6 route.1
  35.8 0.0 collective-permute-done.4.got_ref
  35.8 0.0 copy-done.14
  35.8 0.0 copy-done.15
  35.9 0.0 copy-done.10
  35.9 0.0 copy-start.9
  35.9 3.6 %finish.1 = (f32[256,2048]{1,0:T(8,128)S(1)}, bf16[768,2048]{1,0:T(8,128)(2,1)S(1)}) custom-call(s32[2]{0:T(128)S(1)} %pad_add_fusion.place_ref, f32[256,2048]{1,0:T(8,128)S(1)} %get-tuple-element.13.intra_ref, bf16[256,2048]{1,0:T(8,128)(2,1)S(1)} %bitcast.36, bf16[1024,128]{1,0:T(8,128)(2,1)S(1)} %get-tuple-element.14.keep_ref, ...), custom_call_target="tpu_custom_call" | custom-call | tf_op jit(solution)/shard_map/finish/pallas_call | solution.py:28
  39.5 0.0 copy-start.7
  39.5 0.0 copy-start.8
  39.5 84.9 %all_to_all.10 = bf16[32,24,2048]{2,1,0:T(8,128)(2,1)S(1)} all-to-all(bf16[32,24,2048]{2,1,0:T(8,128)(2,1)S(1)} %bitcast.37), channel_id=1, replica_groups=mesh['seq'=8,'exp'=32] {'exp'}, dimensions={0} | all-to-all | bytes 6291456 | tf_op jit(solution)/shard_map/all_to_all | solution.py:273
  124.5 0.0 copy-done.9
  124.5 0.0 copy-done.7
  124.5 7.5 %expert.1 = bf16[768,2048]{1,0:T(8,128)(2,1)S(1)} custom-call(bf16[768,2048]{1,0:T(8,128)(2,1)S(1)} %bitcast.27, bf16[2048,768]{1,0:T(8,128)(2,1)S(1)} %bitcast.38, bf16[2048,768]{1,0:T(8,128)(2,1)S(1)} %bitcast.39, bf16[768,2048]{1,0:T(8,128)(2,1)S(1)} %bitcast.40), custom_call_target="tpu_custom_call" | custom-call | tf_op jit(solution)/shard_map/expert/pallas_call | solution.py:28
  131.9 78.6 %all_to_all.11 = bf16[32,24,2048]{2,1,0:T(8,128)(2,1)S(1)} all-to-all(bf16[32,24,2048]{2,1,0:T(8,128)(2,1)S(1)} %bitcast.28), channel_id=1, replica_groups=mesh['seq'=8,'exp'=32] {'exp'}, dimensions={0} | all-to-all | bytes 6291456 | tf_op jit(solution)/shard_map/all_to_all | solution.py:281
  210.6 1.0 combine.1
  211.6 1.0 copy.13
  (11 shorter events, 0.0 us)
Async XLA Ops:
  0.0 1.2 copy-start
  1.2 1.2 copy-start.3
  2.5 0.7 copy-start.11
  3.2 28.4 %copy-start.2 = (bf16[1,256,2048]{2,1,0:T(8,128)(2,1)S(1)}, bf16[1,256,2048]{2,1,0:T(8,128)(2,1)}, u32[]{:S(2)}) copy-start(bf16[1,256,2048]{2,1,0:T(8,128)(2,1)} %param.14) | copy-start | bytes 3145732
  3.2 28.4 %copy-start.5 = (bf16[1,256,2048]{2,1,0:T(8,128)(2,1)S(1)}, bf16[1,256,2048]{2,1,0:T(8,128)(2,1)}, u32[]{:S(2)}) copy-start(bf16[1,256,2048]{2,1,0:T(8,128)(2,1)} %param.15) | copy-start | bytes 3145732
  3.2 28.4 %copy-start.13 = (f32[1,256,16]{1,2,0:T(8,128)S(1)}, f32[1,256,16]{1,2,0:T(8,128)}, u32[]{:S(2)}) copy-start(f32[1,256,16]{1,2,0:T(8,128)} %param.16) | copy-start | bytes 49156
  5.1 4.6 %collective-permute-start = (bf16[1056,128]{1,0:T(8,128)(2,1)}, bf16[1056,128]{1,0:T(8,128)(2,1)}, u32[]{:S(2)}, u32[]{:S(2)}) collective-permute-start(bf16[1056,128]{1,0:T(8,128)(2,1)} %contrib.3), channel_id=1, source_target_pairs={{0,32},{32,0},{64,96},{96,64},{128,160},{160,128},{192,224},{224,1... | collective-permute-start | bytes 811016 | tf_op jit(solution)/shard_map/ppermute | solution.py:233
  5.1 1.2 copy-start.1
  6.3 1.2 copy-start.4
  7.6 0.7 copy-start.12
  8.3 23.3 %copy-start.6 = (bf16[1,256,2048]{2,1,0:T(8,128)(2,1)S(1)}, bf16[1,256,2048]{2,1,0:T(8,128)(2,1)}, u32[]{:S(2)}) copy-start(bf16[1,256,2048]{2,1,0:T(8,128)(2,1)} %param.13) | copy-start | bytes 3145732
  9.5 25.6 %copy-start.16 = (s32[1,256,2]{1,2,0:T(2,128)S(1)}, s32[1,256,2]{1,2,0:T(2,128)}, u32[]{:S(2)}) copy-start(s32[1,256,2]{1,2,0:T(2,128)} %param.19) | copy-start | bytes 6148
  9.5 25.6 %copy-start.17 = (s32[1,256,2]{1,2,0:T(2,128)S(1)}, s32[1,256,2]{1,2,0:T(2,128)}, u32[]{:S(2)}) copy-start(s32[1,256,2]{1,2,0:T(2,128)} %param.20) | copy-start | bytes 6148
  9.6 26.3 %copy-start.14 = (f32[2048]{0:T(1024)S(1)}, f32[2048]{0:T(1024)}, u32[]{:S(2)}) copy-start(f32[2048]{0:T(1024)} %param.17) | copy-start | bytes 24580
  9.6 26.3 %copy-start.15 = (f32[2048]{0:T(1024)S(1)}, f32[2048]{0:T(1024)}, u32[]{:S(2)}) copy-start(f32[2048]{0:T(1024)} %param.18) | copy-start | bytes 24580
  9.6 26.3 %copy-start.10 = (bf16[1,256,2048]{2,1,0:T(8,128)(2,1)S(1)}, bf16[1,256,2048]{2,1,0:T(8,128)(2,1)}, u32[]{:S(2)}) copy-start(bf16[1,256,2048]{2,1,0:T(8,128)(2,1)} %param.12) | copy-start | bytes 3145732
  10.9 15.3 %collective-permute-start.3 = (bf16[1056,128]{1,0:T(8,128)(2,1)S(1)}, bf16[1056,128]{1,0:T(8,128)(2,1)S(1)}, u32[]{:S(2)}, u32[]{:S(2)}) collective-permute-start(bf16[1056,128]{1,0:T(8,128)(2,1)S(1)} %pair.1), channel_id=1, source_target_pairs={{0,192},{32,224},{64,0},{96,32},{128,64},{160,96},{192,128},{224,1... | collective-permute-start | bytes 811016 | tf_op jit(solution)/shard_map/ppermute | solution.py:236
  14.0 12.2 %collective-permute-start.2 = (bf16[1056,128]{1,0:T(8,128)(2,1)S(1)}, bf16[1056,128]{1,0:T(8,128)(2,1)S(1)}, u32[]{:S(2)}, u32[]{:S(2)}) collective-permute-start(bf16[1056,128]{1,0:T(8,128)(2,1)S(1)} %pair.1), channel_id=1, source_target_pairs={{0,128},{32,160},{64,192},{96,224},{128,0},{160,32},{192,64},{224,... | collective-permute-start | bytes 811016 | tf_op jit(solution)/shard_map/ppermute | solution.py:236
  14.6 15.3 %collective-permute-start.1 = (bf16[1056,128]{1,0:T(8,128)(2,1)S(1)}, bf16[1056,128]{1,0:T(8,128)(2,1)S(1)}, u32[]{:S(2)}, u32[]{:S(2)}) collective-permute-start(bf16[1056,128]{1,0:T(8,128)(2,1)S(1)} %pair.1), channel_id=1, source_target_pairs={{0,64},{32,96},{64,128},{96,160},{128,192},{160,224},{192,0},{224,... | collective-permute-start | bytes 811016 | tf_op jit(solution)/shard_map/ppermute | solution.py:236
  31.2 4.6 %collective-permute-start.4 = (bf16[1024,128]{1,0:T(8,128)(2,1)S(1)}, bf16[1024,128]{1,0:T(8,128)(2,1)S(1)}, u32[]{:S(2)}, u32[]{:S(2)}) collective-permute-start(bf16[1024,128]{1,0:T(8,128)(2,1)S(1)} %get-tuple-element.15), channel_id=1, source_target_pairs={{0,32},{32,0},{64,96},{96,64},{128,160},{160,128},{192,224},{224,1... | collective-permute-start | bytes 786440 | tf_op jit(solution)/shard_map/ppermute | solution.py:239
  35.9 88.6 %copy-start.9 = (bf16[1,768,2048]{2,1,0:T(8,128)(2,1)S(1)}, bf16[1,768,2048]{2,1,0:T(8,128)(2,1)}, u32[]{:S(2)}) copy-start(bf16[1,768,2048]{2,1,0:T(8,128)(2,1)} %param.23) | copy-start | bytes 9437188
  39.5 84.9 %copy-start.7 = (bf16[1,2048,768]{2,1,0:T(8,128)(2,1)S(1)}, bf16[1,2048,768]{2,1,0:T(8,128)(2,1)}, u32[]{:S(2)}) copy-start(bf16[1,2048,768]{2,1,0:T(8,128)(2,1)} %param.21) | copy-start | bytes 9437188
  39.5 84.9 %copy-start.8 = (bf16[1,2048,768]{2,1,0:T(8,128)(2,1)S(1)}, bf16[1,2048,768]{2,1,0:T(8,128)(2,1)}, u32[]{:S(2)}) copy-start(bf16[1,2048,768]{2,1,0:T(8,128)(2,1)} %param.22) | copy-start | bytes 9437188

commit v3 on v2

--- a/solution.py
+++ b/solution.py
@@ -192,10 +192,23 @@
 
 
 def combine_body(back_ref, h_ref, mix_ref, out_ref):
+    step = out_ref.shape[1]
+    cols = pl.ds(pl.multiple_of(pl.program_id(0) * step, 128), step)
+    out_ref[...] = (h_ref[:, cols] + dot(mix_ref[...], back_ref[:, cols])).astype(BF16)
+
+
+def combine(back, h_res, mix):
+    block, width = h_res.shape
     step = 512
-    for c in range(0, h_ref.shape[1], step):
-        cols = slice(c, c + step)
-        out_ref[:, cols] = (h_ref[:, cols] + dot(mix_ref[...], back_ref[:, cols])).astype(BF16)
+    return pl.pallas_call(
+        combine_body,
+        out_shape=jax.ShapeDtypeStruct((block, width), BF16),
+        grid=(width // step,),
+        in_specs=[VMEM_SPEC] * 3,
+        out_specs=pl.BlockSpec((block, step), lambda i: (0, i)),
+        compiler_params=pltpu.CompilerParams(vmem_limit_bytes=VMEM_LIMIT),
+        name="combine",
+    )(near(back), near(h_res), near(mix))
 
 
 def contribution(half, k, v, decay_t):
@@ -217,24 +230,29 @@
         ),
         compiler_params=pltpu.CompilerParams(vmem_limit_bytes=VMEM_LIMIT),
         name="contrib",
-    )(half, k, v, decay_t)
-
-
-def carried_states(k, v, decay_t, place):
+    )(half, *(pltpu.with_memory_space_constraint(a, pltpu.HBM) for a in (k, v, decay_t)))
+
+
+def pair_states(k, v, decay_t, place):
+    swap = [(i, i ^ 1) for i in range(lax.axis_size("seq"))]
+    core = place[:1]
+    other = lax.ppermute(contribution(1 - core, k, v, decay_t), "seq", swap)
+    own = contribution(core, k, v, decay_t)
+    return own, other, local(pair_body, "pair", [(own.shape, BF16)], own, other, scalars=place)
+
+
+def of_earlier_chips(pair):
     blocks = lax.axis_size("seq")
     chips = blocks // 2
-    dh = k.shape[1] // decay_t.shape[0]
-    core = place[:1]
-    swap = [(i, i ^ 1) for i in range(blocks)]
-
-    def along(by):
-        return [(i, (i // 2 + by) % chips * 2 + i % 2) for i in range(blocks)]
-
-    other = lax.ppermute(contribution(1 - core, k, v, decay_t), "seq", swap)
-    own = contribution(core, k, v, decay_t)
-    pair = local(pair_body, "pair", [(own.shape, BF16)], own, other, scalars=place)
-    earlier = [lax.ppermute(pair, "seq", along(by)) for by in range(1, chips)]
-    half = ((own.shape[0] - LOG_ROWS, dh), BF16)
+    return [
+        lax.ppermute(pair, "seq", [(i, (i // 2 + by) % chips * 2 + i % 2) for i in range(blocks)])
+        for by in range(1, chips)
+    ]
+
+
+def carried_states(own, other, earlier, place):
+    swap = [(i, i ^ 1) for i in range(lax.axis_size("seq"))]
+    half = ((own.shape[0] - LOG_ROWS, own.shape[1]), BF16)
     keep, send = local(carry_body, "carry", [half, half], own, other, *earlier, scalars=place)
     return keep, lax.ppermute(send, "seq", swap)
 
@@ -252,7 +270,9 @@
     index = lax.axis_index("seq")
     place = jnp.stack([index % 2, index // 2]).astype(jnp.int32)
 
-    keep, got = carried_states(k, v, decay_t, place)
+    own, other, pair = pair_states(k, v, decay_t, place)
+    pair, q, ids = lax.optimization_barrier((pair, q, expert_ids[0]))
+    earlier = of_earlier_chips(pair)
     intra, grow = local(
         intra_body, "intra", [((block, width), F32), ((block, heads), F32)], q, k, v, decay_t
     )
@@ -260,9 +280,11 @@
         lambda *refs: route_body(*refs, cap=cap),
         "route",
         [((slots, block), BF16), ((block, slots), BF16)],
-        expert_ids[0].T,
+        ids.T,
         gate_levels[0].T,
     )
+    earlier, intra, grow, pick, mix = lax.optimization_barrier((earlier, intra, grow, pick, mix))
+    keep, got = carried_states(own, other, earlier, place)
     h_res, send = local(
         finish_body,
         "finish",
@@ -279,10 +301,7 @@
         scratch=[pltpu.VMEM((slots, hidden), BF16)],
     )
     back = lax.all_to_all(done.reshape(experts, cap, width), "exp", 0, 0, tiled=True)
-    out = local(
-        combine_body, "combine", [((block, width), BF16)], back.reshape(slots, width), h_res, mix
-    )
-    return out[None]
+    return combine(back.reshape(slots, width), h_res, mix)[None]
 
 
 def solution(mesh):

time: 213 us -> 206 us (0.967)
  local copies, waits for them, and re-layouts: 7.37 us -> 0.06 us
  Pallas kernels: 22 us -> 26.1 us
  waiting for transfers between devices: 14.3 us -> 11.6 us
    unnamed x37 -> x24, local copies, waits for them, and re-layouts: 7.37 us -> 0.06 us
    ppermute x4, waiting for transfers between devices: 14.3 us -> 10 us  [the longest x3 10 us: of_earlier_chips(): lax.ppermute(pair, 'seq', [(i, (i // 2 + by) % chips * 2 + i % 2) for i i...]
    pallas_call x0 -> x1, Pallas kernels: none -> 2.54 us  [combine(): pl.pallas_call(combine_body, out_shape=jax.ShapeDtypeStruct((block, width...]
    pallas_call x2, Pallas kernels: 3.18 us -> 5.7 us  [contribution(): pl.pallas_call(contrib_body, out_shape=pltpu.VMEM((width // 2 + LOG_ROWS,...]
    pallas_call x7 -> x6, Pallas kernels: 18.9 us -> 17.9 us  [local(): pl.pallas_call(body, out_shape=tuple((pltpu.VMEM(shape, dtype) for shape,...]
  transfers between devices with their start and end apart: 5 -> 5, of which waited for: 2 -> 3; matrix products, arithmetic and copies ran while one was open for 0% -> 0% of each run, Pallas kernels for 3% -> 3%
where the time goes in v3:
time: 206 us
  blocking collectives  163 us (79%)
  Pallas kernels  26.1 us (13%)
  waiting for transfers between devices  11.6 us (6%)
  starting transfers between devices  4.98 us (2%)
    all_to_all x1, blocking collectives, per_device(): lax.all_to_all(send.reshape(experts, cap, width), 'exp', 0, 0, tiled=True)  85 us
    all_to_all x1, blocking collectives, per_device(): lax.all_to_all(done.reshape(experts, cap, width), 'exp', 0, 0, tiled=True)  77.9 us
    pallas_call x6, Pallas kernels, local(): pl.pallas_call(body, out_shape=tuple((pltpu.VMEM(shape, dtype) for shape,...  17.9 us
    ppermute x3, waiting for transfers between devices, of_earlier_chips(): lax.ppermute(pair, 'seq', [(i, (i // 2 + by) % chips * 2 + i % 2) for i i...  10 us
    pallas_call x2, Pallas kernels, contribution(): pl.pallas_call(contrib_body, out_shape=pltpu.VMEM((width // 2 + LOG_ROWS,...  5.7 us
    ppermute x3, starting transfers between devices, of_earlier_chips(): lax.ppermute(pair, 'seq', [(i, (i // 2 + by) % chips * 2 + i % 2) for i i...  4.69 us
  transfers between devices with their start and end apart: 5, of which 3 were waited for; matrix products, arithmetic and copies ran while one was open for 0% of the time, Pallas kernels for 3%

profile of v3, /device:TPU:32, one launch (start us, length us, event | category | flops | bytes accessed | tf_op | source)
XLA Modules:
  0.0 205.9 jit_solution(5252034670714718154)
XLA Ops:
  0.0 0.0 copy-start.7
  0.0 0.0 copy-start.1
  0.0 0.0 copy-start
  0.0 0.0 copy-start.2
  0.0 3.3 %contrib.3 = bf16[1056,128]{1,0:T(8,128)(2,1)} custom-call(s32[1]{0:T(128)S(6)} %sub.8.half_ref, bf16[256,2048]{1,0:T(8,128)(2,1)} %bitcast.27, bf16[256,2048]{1,0:T(8,128)(2,1)} %bitcast.30, f32[16,256]{1,0:T(8,128)} %bitcast.40), custom_call_target="tpu_custom_call" | custom-call | tf_op jit(solution)/shard_map/contrib/pallas_call | solution.py:218
  3.3 0.0 collective-permute-start
  3.3 0.0 copy-start.10
  3.3 0.0 copy-start.11
  3.3 2.4 %contrib.2.own_ref = bf16[1056,128]{1,0:T(8,128)(2,1)S(1)} custom-call(s32[1]{0:T(128)} %bitcast.half_ref, bf16[256,2048]{1,0:T(8,128)(2,1)} %bitcast.28, bf16[256,2048]{1,0:T(8,128)(2,1)} %bitcast.31, f32[16,256]{1,0:T(8,128)} %bitcast.41), custom_call_target="tpu_custom_call" | custom-call | tf_op jit(solution)/shard_map/contrib/pallas_call | solution.py:218
  5.7 0.0 copy-start.8
  5.8 0.0 copy-start.9
  5.8 0.0 copy-start.6
  5.8 0.1 pad_add_fusion.place_ref
  5.9 0.0 collective-permute-done.other_ref
  5.9 1.2 pair.1
  7.1 3.1 %collective-permute-start.3 = (bf16[1056,128]{1,0:T(8,128)(2,1)S(1)}, bf16[1056,128]{1,0:T(8,128)(2,1)S(1)}, u32[]{:S(2)}, u32[]{:S(2)}) collective-permute-start(bf16[1056,128]{1,0:T(8,128)(2,1)S(1)} %pair.1), channel_id=1, source_target_pairs={{0,192},{32,224},{64,0},{96,32},{128,64},{160,96},{192,128},{224,1... | collective-permute-start | bytes 811016 | tf_op jit(solution)/shard_map/ppermute | solution.py:248
  10.2 0.6 collective-permute-start.2
  10.8 1.0 collective-permute-start.1
  11.8 0.0 copy-done.7
  11.8 0.0 copy-done.1
  11.8 0.0 copy-done
  11.8 0.0 copy-done.2
  11.8 3.6 %intra.1 = (f32[256,2048]{1,0:T(8,128)S(1)}, f32[256,16]{1,0:T(8,128)S(1)}) custom-call(bf16[256,2048]{1,0:T(8,128)(2,1)S(1)} %bitcast.33, bf16[256,2048]{1,0:T(8,128)(2,1)S(1)} %bitcast.29, bf16[256,2048]{1,0:T(8,128)(2,1)S(1)} %bitcast.32, f32[16,256]{1,0:T(8,128)S(1)} %bitcast.42), custom_call_target="tpu_custom_call" | custom-call | tf_op jit(solution)/shard_map/intra/pallas_call | solution.py:28
  15.4 0.0 copy-done.10
  15.4 0.0 copy-done.11
  15.4 0.6 route.1
  16.1 6.3 %collective-permute-done.3.refs_2_ = bf16[1056,128]{1,0:T(8,128)(2,1)S(1)} collective-permute-done((bf16[1056,128]{1,0:T(8,128)(2,1)S(1)}, bf16[1056,128]{1,0:T(8,128)(2,1)S(1)}, u32[]{:S(2)}, u32[]{:S(2)}) %collective-permute-start.3) | collective-permute-done | bytes 270368 | tf_op jit(solution)/shard_map/ppermute | solution.py:248
  22.4 0.0 collective-permute-done.2.refs_1_
  22.4 3.7 %collective-permute-done.1.refs_0_ = bf16[1056,128]{1,0:T(8,128)(2,1)S(1)} collective-permute-done((bf16[1056,128]{1,0:T(8,128)(2,1)S(1)}, bf16[1056,128]{1,0:T(8,128)(2,1)S(1)}, u32[]{:S(2)}, u32[]{:S(2)}) %collective-permute-start.1) | collective-permute-done | bytes 270368 | tf_op jit(solution)/shard_map/ppermute | solution.py:248
  26.1 1.3 carry.1
  27.4 0.3 collective-permute-start.4
  27.7 1.5 collective-permute-done.4.got_ref
  29.2 0.0 copy-done.8
  29.2 0.0 copy-done.9
  29.2 0.0 copy-done.6
  29.2 0.0 copy-start.5
  29.3 3.6 %finish.1 = (f32[256,2048]{1,0:T(8,128)S(1)}, bf16[768,2048]{1,0:T(8,128)(2,1)S(1)}) custom-call(s32[2]{0:T(128)S(1)} %pad_add_fusion.place_ref, f32[256,2048]{1,0:T(8,128)S(1)} %get-tuple-element.30.intra_ref, bf16[256,2048]{1,0:T(8,128)(2,1)S(1)} %bitcast.34, bf16[1024,128]{1,0:T(8,128)(2,1)S(1)} %get-tuple-element.34.keep_ref, ...), custom_call_target="tpu_custom_call" | custom-call | tf_op jit(solution)/shard_map/finish/pallas_call | solution.py:28
  32.9 0.0 copy-start.3
  32.9 0.0 copy-start.4
  32.9 85.0 %all_to_all.10 = bf16[32,24,2048]{2,1,0:T(8,128)(2,1)S(1)} all-to-all(bf16[32,24,2048]{2,1,0:T(8,128)(2,1)S(1)} %bitcast.35), channel_id=1, replica_groups=mesh['seq'=8,'exp'=32] {'exp'}, dimensions={0} | all-to-all | bytes 6291456 | tf_op jit(solution)/shard_map/all_to_all | solution.py:295
  117.9 0.0 copy-done.5
  117.9 0.0 copy-done.3
  117.9 0.0 copy-done.4
  117.9 7.5 %expert.1 = bf16[768,2048]{1,0:T(8,128)(2,1)S(1)} custom-call(bf16[768,2048]{1,0:T(8,128)(2,1)S(1)} %bitcast.25, bf16[2048,768]{1,0:T(8,128)(2,1)S(1)} %bitcast.36, bf16[2048,768]{1,0:T(8,128)(2,1)S(1)} %bitcast.37, bf16[768,2048]{1,0:T(8,128)(2,1)S(1)} %bitcast.38), custom_call_target="tpu_custom_call" | custom-call | tf_op jit(solution)/shard_map/expert/pallas_call | solution.py:28
  125.4 77.9 %all_to_all.11 = bf16[32,24,2048]{2,1,0:T(8,128)(2,1)S(1)} all-to-all(bf16[32,24,2048]{2,1,0:T(8,128)(2,1)S(1)} %bitcast.26), channel_id=1, replica_groups=mesh['seq'=8,'exp'=32] {'exp'}, dimensions={0} | all-to-all | bytes 6291456 | tf_op jit(solution)/shard_map/all_to_all | solution.py:303
  203.3 2.5 %combine.1 = bf16[256,2048]{1,0:T(8,128)(2,1)} custom-call(bf16[768,2048]{1,0:T(8,128)(2,1)S(1)} %bitcast.24, f32[256,2048]{1,0:T(8,128)S(1)} %get-tuple-element.39.h_ref, bf16[256,768]{1,0:T(8,128)(2,1)S(1)} %get-tuple-element.40.mix_ref), custom_call_target="tpu_custom_call" | custom-call | tf_op jit(solution)/shard_map/combine/pallas_call | solution.py:203
Async XLA Ops:
  0.0 11.8 %copy-start.7 = (f32[1,256,16]{1,2,0:T(8,128)S(1)}, f32[1,256,16]{1,2,0:T(8,128)}, u32[]{:S(2)}) copy-start(f32[1,256,16]{1,2,0:T(8,128)} %param.16) | copy-start | bytes 49156
  0.0 11.8 %copy-start.1 = (bf16[1,256,2048]{2,1,0:T(8,128)(2,1)S(1)}, bf16[1,256,2048]{2,1,0:T(8,128)(2,1)}, u32[]{:S(2)}) copy-start(bf16[1,256,2048]{2,1,0:T(8,128)(2,1)} %param.15) | copy-start | bytes 3145732
  0.0 11.8 %copy-start = (bf16[1,256,2048]{2,1,0:T(8,128)(2,1)S(1)}, bf16[1,256,2048]{2,1,0:T(8,128)(2,1)}, u32[]{:S(2)}) copy-start(bf16[1,256,2048]{2,1,0:T(8,128)(2,1)} %param.14) | copy-start | bytes 3145732
  0.0 11.8 %copy-start.2 = (bf16[1,256,2048]{2,1,0:T(8,128)(2,1)S(1)}, bf16[1,256,2048]{2,1,0:T(8,128)(2,1)}, u32[]{:S(2)}) copy-start(bf16[1,256,2048]{2,1,0:T(8,128)(2,1)} %param.13) | copy-start | bytes 3145732
  3.3 2.6 %collective-permute-start = (bf16[1056,128]{1,0:T(8,128)(2,1)}, bf16[1056,128]{1,0:T(8,128)(2,1)}, u32[]{:S(2)}, u32[]{:S(2)}) collective-permute-start(bf16[1056,128]{1,0:T(8,128)(2,1)} %contrib.3), channel_id=1, source_target_pairs={{0,32},{32,0},{64,96},{96,64},{128,160},{160,128},{192,224},{224,1... | collective-permute-start | bytes 811016 | tf_op jit(solution)/shard_map/ppermute | solution.py:239
  3.3 12.1 %copy-start.10 = (s32[1,256,2]{1,2,0:T(2,128)S(1)}, s32[1,256,2]{1,2,0:T(2,128)}, u32[]{:S(2)}) copy-start(s32[1,256,2]{1,2,0:T(2,128)} %param.19) | copy-start | bytes 6148
  3.3 12.1 %copy-start.11 = (s32[1,256,2]{1,2,0:T(2,128)S(1)}, s32[1,256,2]{1,2,0:T(2,128)}, u32[]{:S(2)}) copy-start(s32[1,256,2]{1,2,0:T(2,128)} %param.20) | copy-start | bytes 6148
  5.7 23.5 %copy-start.8 = (f32[2048]{0:T(1024)S(1)}, f32[2048]{0:T(1024)}, u32[]{:S(2)}) copy-start(f32[2048]{0:T(1024)} %param.17) | copy-start | bytes 24580
  5.8 23.5 %copy-start.9 = (f32[2048]{0:T(1024)S(1)}, f32[2048]{0:T(1024)}, u32[]{:S(2)}) copy-start(f32[2048]{0:T(1024)} %param.18) | copy-start | bytes 24580
  5.8 23.4 %copy-start.6 = (bf16[1,256,2048]{2,1,0:T(8,128)(2,1)S(1)}, bf16[1,256,2048]{2,1,0:T(8,128)(2,1)}, u32[]{:S(2)}) copy-start(bf16[1,256,2048]{2,1,0:T(8,128)(2,1)} %param.12) | copy-start | bytes 3145732
  7.1 15.3 %collective-permute-start.3 = (bf16[1056,128]{1,0:T(8,128)(2,1)S(1)}, bf16[1056,128]{1,0:T(8,128)(2,1)S(1)}, u32[]{:S(2)}, u32[]{:S(2)}) collective-permute-start(bf16[1056,128]{1,0:T(8,128)(2,1)S(1)} %pair.1), channel_id=1, source_target_pairs={{0,192},{32,224},{64,0},{96,32},{128,64},{160,96},{192,128},{224,1... | collective-permute-start | bytes 811016 | tf_op jit(solution)/shard_map/ppermute | solution.py:248
  10.2 12.2 %collective-permute-start.2 = (bf16[1056,128]{1,0:T(8,128)(2,1)S(1)}, bf16[1056,128]{1,0:T(8,128)(2,1)S(1)}, u32[]{:S(2)}, u32[]{:S(2)}) collective-permute-start(bf16[1056,128]{1,0:T(8,128)(2,1)S(1)} %pair.1), channel_id=1, source_target_pairs={{0,128},{32,160},{64,192},{96,224},{128,0},{160,32},{192,64},{224,... | collective-permute-start | bytes 811016 | tf_op jit(solution)/shard_map/ppermute | solution.py:248
  10.8 15.3 %collective-permute-start.1 = (bf16[1056,128]{1,0:T(8,128)(2,1)S(1)}, bf16[1056,128]{1,0:T(8,128)(2,1)S(1)}, u32[]{:S(2)}, u32[]{:S(2)}) collective-permute-start(bf16[1056,128]{1,0:T(8,128)(2,1)S(1)} %pair.1), channel_id=1, source_target_pairs={{0,64},{32,96},{64,128},{96,160},{128,192},{160,224},{192,0},{224,... | collective-permute-start | bytes 811016 | tf_op jit(solution)/shard_map/ppermute | solution.py:248
  27.4 1.8 collective-permute-start.4
  29.2 88.7 %copy-start.5 = (bf16[1,768,2048]{2,1,0:T(8,128)(2,1)S(1)}, bf16[1,768,2048]{2,1,0:T(8,128)(2,1)}, u32[]{:S(2)}) copy-start(bf16[1,768,2048]{2,1,0:T(8,128)(2,1)} %param.23) | copy-start | bytes 9437188
  32.9 85.0 %copy-start.3 = (bf16[1,2048,768]{2,1,0:T(8,128)(2,1)S(1)}, bf16[1,2048,768]{2,1,0:T(8,128)(2,1)}, u32[]{:S(2)}) copy-start(bf16[1,2048,768]{2,1,0:T(8,128)(2,1)} %param.21) | copy-start | bytes 9437188
  32.9 85.0 %copy-start.4 = (bf16[1,2048,768]{2,1,0:T(8,128)(2,1)S(1)}, bf16[1,2048,768]{2,1,0:T(8,128)(2,1)}, u32[]{:S(2)}) copy-start(bf16[1,2048,768]{2,1,0:T(8,128)(2,1)} %param.22) | copy-start | bytes 9437188

commit v4 on v3

--- a/solution.py
+++ b/solution.py
@@ -20,20 +20,24 @@
     return pltpu.with_memory_space_constraint(x, pltpu.VMEM)
 
 
-def local(body, name, outs, *args, scalars=None, scratch=()):
-    specs = [VMEM_SPEC] * len(args)
-    given = [near(a) for a in args]
-    if scalars is not None:
-        specs, given = [SMEM_SPEC, *specs], [scalars, *given]
+def far(x):
+    return pltpu.with_memory_space_constraint(x, pltpu.HBM)
+
+
+def local(body, name, outs, *args, scalars=(), scratch=()):
     made = pl.pallas_call(
         body,
         out_shape=tuple(pltpu.VMEM(shape, dtype) for shape, dtype in outs),
-        in_specs=specs,
-        out_specs=tuple(VMEM_SPEC for _ in outs),
-        scratch_shapes=list(scratch),
+        grid_spec=pltpu.PrefetchScalarGridSpec(
+            num_scalar_prefetch=len(scalars),
+            grid=(1,),
+            in_specs=[VMEM_SPEC] * len(args),
+            out_specs=tuple(VMEM_SPEC for _ in outs),
+            scratch_shapes=list(scratch),
+        ),
         compiler_params=pltpu.CompilerParams(vmem_limit_bytes=VMEM_LIMIT),
         name=name,
-    )(*given)
+    )(*scalars, *(near(a) for a in args))
     return made[0] if len(outs) == 1 else made
 
 
@@ -64,26 +68,36 @@
     return a + b + c
 
 
-def contrib_body(half_ref, k_ref, v_ref, decay_ref, out_ref):
+def contrib_body(half_ref, k_ref, v_ref, decay_ref, out_ref, decayed_ref):
     heads, block = decay_ref.shape
-    dh = k_ref.shape[1] // heads
-    lower = (iota((block, block), 0) >= iota((block, block), 1)).astype(F32)
-    cum = -dot(lower, decay_ref[...], 1, 1, precision=EXACT)
-    total = cum[block - 1 : block, :]
-    decayed = jnp.exp(total - cum)
-    logs = []
-    for h in range(heads):
-        cols = slice(h * dh, (h + 1) * dh)
-        kw = (k_ref[:, cols].astype(F32) * decayed[:, h : h + 1]).astype(BF16)
-        out_ref[cols, :] = dot(kw, v_ref[:, cols], 0, 0).astype(BF16)
-        logs.append(jnp.broadcast_to(total[:, h : h + 1], (1, dh)))
-    out_ref[heads * dh :, :] = log_rows(logs, dh)
-
-
-def pair_body(place_ref, own_ref, other_ref, out_ref):
+    steps = pl.num_programs(0)
+    dh = out_ref.shape[1]
+    per = k_ref.shape[1] // dh
+    step = pl.program_id(0)
+
+    @pl.when(step == 0)
+    def _():
+        lower = (iota((block, block), 0) >= iota((block, block), 1)).astype(F32)
+        cum = -dot(lower, decay_ref[...], 1, 1, precision=EXACT)
+        total = cum[block - 1 : block, :]
+        decayed_ref[...] = jnp.exp(total - cum)
+        logs = [jnp.broadcast_to(total[:, h : h + 1], (1, dh)) for h in range(heads)]
+        out_ref[heads * dh :, :] = log_rows(logs, dh)
+
+    for i in range(per):
+        cols = slice(i * dh, (i + 1) * dh)
+        weight = decayed_ref[:, i : i + 1]
+        for later in range(per, heads, per):
+            weight = jnp.where(step == later // per, decayed_ref[:, later + i : later + i + 1], weight)
+        kw = (k_ref[:, cols].astype(F32) * weight).astype(BF16)
+        rows = pl.ds(pl.multiple_of((step * per + i) * dh, dh), dh)
+        out_ref[rows, :] = dot(kw, v_ref[:, cols], 0, 0).astype(BF16)
+
+
+def pair_body(core_ref, own_ref, other_ref, out_ref):
     dh = own_ref.shape[1]
     heads = (own_ref.shape[0] - LOG_ROWS) // dh
-    is_even = place_ref[0] == 0
+    is_even = core_ref[0] == 0
     logs = []
     for h in range(heads):
         rows = slice(h * dh, (h + 1) * dh)
@@ -95,12 +109,12 @@
     out_ref[heads * dh :, :] = log_rows(logs, dh)
 
 
-def carry_body(place_ref, own_ref, other_ref, *refs):
+def carry_body(core_ref, chip_ref, own_ref, other_ref, *refs):
     *earlier, keep_ref, send_ref = refs
     dh = own_ref.shape[1]
     heads = keep_ref.shape[0] // dh
-    is_even = place_ref[0] == 0
-    chip = place_ref[1]
+    is_even = core_ref[0] == 0
+    chip = chip_ref[0]
     for h in range(heads):
         rows = slice(h * dh, (h + 1) * dh)
         state = jnp.zeros((dh, dh), F32)
@@ -123,7 +137,8 @@
     decay = decay_ref[...]
     cum = -dot(lower, decay, 1, 1, precision=EXACT)
     cum_t = -dot(decay, lower, 1, 1, precision=EXACT)
-    grow_ref[...] = jnp.exp(cum)
+    part = pl.program_id(0)
+    grow_ref[part] = jnp.exp(cum)
     for h in range(heads):
         cols = slice(h * dh, (h + 1) * dh)
         for lo, hi in ((0, half), (half, block)):
@@ -131,7 +146,7 @@
             gap = cum[lo:hi, h : h + 1] - cum_t[h : h + 1, :hi]
             seen = iota((hi - lo, hi), 0) + lo >= iota((hi - lo, hi), 1)
             probs = jnp.where(seen, scores * jnp.exp(jnp.minimum(gap, 0.0)), 0.0).astype(BF16)
-            out_ref[lo:hi, cols] = dot(probs, v_ref[:hi, cols])
+            out_ref[part, lo:hi, cols] = dot(probs, v_ref[:hi, cols])
 
 
 def route_body(ids_ref, levels_ref, pick_ref, mix_ref, *, cap):
@@ -153,19 +168,19 @@
 
 
 def finish_body(
-    place_ref, intra_ref, q_ref, keep_ref, got_ref, grow_ref, x_ref, attn_gain_ref, norm_gain_ref, pick_ref, h_ref, send_ref
+    core_ref, intra_ref, q_ref, keep_ref, got_ref, grow_ref, x_ref, attn_gain_ref, norm_gain_ref, pick_ref, h_ref, send_ref
 ):
-    block, heads = grow_ref.shape
-    width = q_ref.shape[1]
+    block, width = q_ref.shape
+    per = grow_ref.shape[2]
+    heads = 2 * per
     dh = width // heads
-    per = heads // 2
-    core = place_ref[0]
+    core = core_ref[0]
     squares = jnp.zeros((block, dh), F32)
     for h in range(heads):
         cols = slice(h * dh, (h + 1) * dh)
         rows = slice(h % per * dh, (h % per + 1) * dh)
         state = jnp.where(core == h // per, keep_ref[rows, :].astype(F32), got_ref[rows, :].astype(F32))
-        raw = intra_ref[:, cols] + grow_ref[:, h : h + 1] * dot(q_ref[:, cols], state.astype(BF16))
+        raw = intra_ref[h // per, :, rows] + grow_ref[h // per, :, h % per : h % per + 1] * dot(q_ref[:, cols], state.astype(BF16))
         scale = lax.rsqrt(jnp.mean(raw * raw, axis=-1, keepdims=True) + 1e-06)
         res = x_ref[:, cols].astype(F32) + attn_gain_ref[:, cols] * (raw * scale)
         h_ref[:, cols] = res
@@ -191,54 +206,72 @@
         out_ref[:, cols] = dot(act_ref[...], down_ref[:, cols]).astype(BF16)
 
 
-def combine_body(back_ref, h_ref, mix_ref, out_ref):
-    step = out_ref.shape[1]
-    cols = pl.ds(pl.multiple_of(pl.program_id(0) * step, 128), step)
-    out_ref[...] = (h_ref[:, cols] + dot(mix_ref[...], back_ref[:, cols])).astype(BF16)
+def combine_body(back_ref, h_ref, mix_ref, out_ref, buf, sems):
+    parts, _, step = buf.shape
+    stores = []
+    for i in range(parts):
+        cols = slice(i * step, (i + 1) * step)
+        buf[i] = (h_ref[:, cols] + dot(mix_ref[...], back_ref[:, cols])).astype(BF16)
+        stores.append(pltpu.make_async_copy(buf.at[i], out_ref.at[:, cols], sems.at[i]))
+        stores[i].start()
+    for store in stores:
+        store.wait()
 
 
 def combine(back, h_res, mix):
     block, width = h_res.shape
-    step = 512
+    parts = 4
     return pl.pallas_call(
         combine_body,
         out_shape=jax.ShapeDtypeStruct((block, width), BF16),
-        grid=(width // step,),
         in_specs=[VMEM_SPEC] * 3,
-        out_specs=pl.BlockSpec((block, step), lambda i: (0, i)),
+        out_specs=pl.BlockSpec(memory_space=pltpu.HBM),
+        scratch_shapes=[pltpu.VMEM((parts, block, width // parts), BF16), pltpu.SemaphoreType.DMA((parts,))],
         compiler_params=pltpu.CompilerParams(vmem_limit_bytes=VMEM_LIMIT),
         name="combine",
     )(near(back), near(h_res), near(mix))
 
 
-def contribution(half, k, v, decay_t):
+def contribution(half, k, v, decay_t, steps=1):
     heads, block = decay_t.shape
     width = k.shape[1]
     dh = width // heads
+    columns = pl.BlockSpec((block, width // 2 // steps), lambda i, half: (0, half[0] * steps + i))
     return pl.pallas_call(
         contrib_body,
         out_shape=pltpu.VMEM((width // 2 + LOG_ROWS, dh), BF16),
         grid_spec=pltpu.PrefetchScalarGridSpec(
             num_scalar_prefetch=1,
-            grid=(1,),
-            in_specs=[
-                pl.BlockSpec((block, width // 2), lambda i, half: (0, half[0])),
-                pl.BlockSpec((block, width // 2), lambda i, half: (0, half[0])),
-                pl.BlockSpec((heads // 2, block), lambda i, half: (half[0], 0)),
-            ],
+            grid=(steps,),
+            in_specs=[columns, columns, pl.BlockSpec((heads // 2, block), lambda i, half: (half[0], 0))],
             out_specs=VMEM_SPEC,
+            scratch_shapes=[pltpu.VMEM((block, heads // 2), F32)],
         ),
         compiler_params=pltpu.CompilerParams(vmem_limit_bytes=VMEM_LIMIT),
         name="contrib",
-    )(half, *(pltpu.with_memory_space_constraint(a, pltpu.HBM) for a in (k, v, decay_t)))
-
-
-def pair_states(k, v, decay_t, place):
+    )(half, far(k), far(v), far(decay_t))
+
+
+def inside_block(q, k, v, decay_t):
+    heads, block = decay_t.shape
+    width = q.shape[1]
+    columns = pl.BlockSpec((block, width // 2), lambda i: (0, i))
+    return pl.pallas_call(
+        intra_body,
+        out_shape=(pltpu.VMEM((2, block, width // 2), F32), pltpu.VMEM((2, block, heads // 2), F32)),
+        grid=(2,),
+        in_specs=[columns, columns, columns, pl.BlockSpec((heads // 2, block), lambda i: (i, 0))],
+        out_specs=(VMEM_SPEC, VMEM_SPEC),
+        compiler_params=pltpu.CompilerParams(vmem_limit_bytes=VMEM_LIMIT),
+        name="intra",
+    )(far(q), far(k), far(v), far(decay_t))
+
+
+def pair_states(k, v, decay_t, core):
     swap = [(i, i ^ 1) for i in range(lax.axis_size("seq"))]
-    core = place[:1]
     other = lax.ppermute(contribution(1 - core, k, v, decay_t), "seq", swap)
     own = contribution(core, k, v, decay_t)
-    return own, other, local(pair_body, "pair", [(own.shape, BF16)], own, other, scalars=place)
+    return own, other, local(pair_body, "pair", [(own.shape, BF16)], own, other, scalars=(core,))
 
 
 def of_earlier_chips(pair):
@@ -250,10 +283,10 @@
     ]
 
 
-def carried_states(own, other, earlier, place):
+def carried_states(own, other, earlier, core, chip):
     swap = [(i, i ^ 1) for i in range(lax.axis_size("seq"))]
     half = ((own.shape[0] - LOG_ROWS, own.shape[1]), BF16)
-    keep, send = local(carry_body, "carry", [half, half], own, other, *earlier, scalars=place)
+    keep, send = local(carry_body, "carry", [half, half], own, other, *earlier, scalars=(core, chip))
     return keep, lax.ppermute(send, "seq", swap)
 
 
@@ -267,15 +300,13 @@
     cap = 3 * block // experts
     slots = experts * cap
     hidden = w_gate.shape[2]
-    index = lax.axis_index("seq")
-    place = jnp.stack([index % 2, index // 2]).astype(jnp.int32)
-
-    own, other, pair = pair_states(k, v, decay_t, place)
+    index = lax.axis_index("seq").reshape(1)
+    core, chip = index & 1, index >> 1
+
+    own, other, pair = pair_states(k, v, decay_t, core)
     pair, q, ids = lax.optimization_barrier((pair, q, expert_ids[0]))
     earlier = of_earlier_chips(pair)
-    intra, grow = local(
-        intra_body, "intra", [((block, width), F32), ((block, heads), F32)], q, k, v, decay_t
-    )
+    intra, grow = inside_block(q, k, v, decay_t)
     pick, mix = local(
         lambda *refs: route_body(*refs, cap=cap),
         "route",
@@ -284,13 +315,13 @@
         gate_levels[0].T,
     )
     earlier, intra, grow, pick, mix = lax.optimization_barrier((earlier, intra, grow, pick, mix))
-    keep, got = carried_states(own, other, earlier, place)
+    keep, got = carried_states(own, other, earlier, core, chip)
     h_res, send = local(
         finish_body,
         "finish",
         [((block, width), F32), ((slots, width), BF16)],
         *(intra, q, keep, got, grow, x, attn_gain[None], norm_gain[None], pick),
-        scalars=place,
+        scalars=(core,),
     )
     arrived = lax.all_to_all(send.reshape(experts, cap, width), "exp", 0, 0, tiled=True)
     done = local(

time: 206 us -> 203 us (0.985)
    pallas_call x0 -> x1, Pallas kernels: none -> 5.55 us  [inside_block(): pl.pallas_call(intra_body, out_shape=(pltpu.VMEM((2, block, width // 2),...]
    pallas_call x6 -> x5, Pallas kernels: 17.9 us -> 12.5 us  [local(): pl.pallas_call(body, out_shape=tuple((pltpu.VMEM(shape, dtype) for shape,...]
  transfers between devices with their start and end apart: 5 -> 5, of which waited for: 3 -> 3; matrix products, arithmetic and copies ran while one was open for 0% -> 0% of each run, Pallas kernels for 3% -> 4%
where the time goes in v4:
time: 203 us; the launch traced here: 202 us
  blocking collectives  163 us (80%)
  Pallas kernels  24.6 us (12%)
  waiting for transfers between devices  9.81 us (5%)
  starting transfers between devices  4.81 us (2%)
    all_to_all x1, blocking collectives, per_device(): lax.all_to_all(send.reshape(experts, cap, width), 'exp', 0, 0, tiled=True)  85 us
    all_to_all x1, blocking collectives, per_device(): lax.all_to_all(done.reshape(experts, cap, width), 'exp', 0, 0, tiled=True)  77.9 us
    pallas_call x5, Pallas kernels, local(): pl.pallas_call(body, out_shape=tuple((pltpu.VMEM(shape, dtype) for shape,...  12.5 us
    ppermute x3, waiting for transfers between devices, of_earlier_chips(): lax.ppermute(pair, 'seq', [(i, (i // 2 + by) % chips * 2 + i % 2) for i i...  8.29 us
    pallas_call x1, Pallas kernels, inside_block(): pl.pallas_call(intra_body, out_shape=(pltpu.VMEM((2, block, width // 2),...  5.55 us
    pallas_call x2, Pallas kernels, contribution(): pl.pallas_call(contrib_body, out_shape=pltpu.VMEM((width // 2 + LOG_ROWS,...  4.83 us
    ppermute x3, starting transfers between devices, of_earlier_chips(): lax.ppermute(pair, 'seq', [(i, (i // 2 + by) % chips * 2 + i % 2) for i i...  4.61 us
  transfers between devices with their start and end apart: 5, of which 3 were waited for; matrix products, arithmetic and copies ran while one was open for 0% of the time, Pallas kernels for 4%

profile of v4, /device:TPU:32, one launch (start us, length us, event | category | flops | bytes accessed | tf_op | source)
XLA Modules:
  0.0 202.5 jit_solution(2396716867835976765)
XLA Ops:
  0.0 2.4 %contrib.3 = bf16[1056,128]{1,0:T(8,128)(2,1)S(1)} custom-call(s32[1]{0:T(128)S(6)} %sub.3.half_ref, bf16[256,2048]{1,0:T(8,128)(2,1)} %bitcast.38, bf16[256,2048]{1,0:T(8,128)(2,1)} %bitcast.41, f32[16,256]{1,0:T(8,128)} %bitcast.44), custom_call_target="tpu_custom_call" | custom-call | tf_op jit(solution)/shard_map/contrib/pallas_call | solution.py:240
  2.4 0.0 copy-start.7
  2.4 0.0 copy-start.8
  2.4 0.1 collective-permute-start
  2.5 2.4 %contrib.2.own_ref = bf16[1056,128]{1,0:T(8,128)(2,1)S(1)} custom-call(s32[1]{0:T(128)} %bitcast.half_ref.core_ref, bf16[256,2048]{1,0:T(8,128)(2,1)} %bitcast.39, bf16[256,2048]{1,0:T(8,128)(2,1)} %bitcast.42, f32[16,256]{1,0:T(8,128)} %bitcast.45), custom_call_target="tpu_custom_call" | custom-call | tf_op jit(solution)/shard_map/contrib/pallas_call | solution.py:240
  5.0 0.0 copy-start
  5.0 0.0 copy-start.4
  5.0 0.0 copy-start.5
  5.0 0.0 copy-start.6
  5.0 0.0 collective-permute-done.other_ref
  5.0 0.9 pair.1
  5.9 3.0 %collective-permute-start.3 = (bf16[1056,128]{1,0:T(8,128)(2,1)}, bf16[1056,128]{1,0:T(8,128)(2,1)S(1)}, u32[]{:S(2)}, u32[]{:S(2)}) collective-permute-start(bf16[1056,128]{1,0:T(8,128)(2,1)} %pair.1), channel_id=1, source_target_pairs={{0,192},{32,224},{64,0},{96,32},{128,64},{160,96},{192,128},{224,1... | collective-permute-start | bytes 811016 | tf_op jit(solution)/shard_map/ppermute | solution.py:281
  8.9 0.6 collective-permute-start.2
  9.5 1.0 collective-permute-start.1
  10.5 5.5 %intra.1 = (f32[2,256,1024]{2,1,0:T(8,128)S(1)}, f32[2,256,8]{2,1,0:T(8,128)S(1)}) custom-call(bf16[256,2048]{1,0:T(8,128)(2,1)} %bitcast.27, bf16[256,2048]{1,0:T(8,128)(2,1)} %bitcast.40, bf16[256,2048]{1,0:T(8,128)(2,1)} %bitcast.43, f32[16,256]{1,0:T(8,128)} %bitcast.46), custom_call_target="tpu_custom_call" | custom-call | tf_op jit(solution)/shard_map/intra/pallas_call | solution.py:259
  16.1 0.0 copy-done.7
  16.1 0.0 copy-done.8
  16.1 0.6 route.1
  16.7 4.7 %collective-permute-done.3.refs_2_ = bf16[1056,128]{1,0:T(8,128)(2,1)S(1)} collective-permute-done((bf16[1056,128]{1,0:T(8,128)(2,1)}, bf16[1056,128]{1,0:T(8,128)(2,1)S(1)}, u32[]{:S(2)}, u32[]{:S(2)}) %collective-permute-start.3) | collective-permute-done | bytes 270368 | tf_op jit(solution)/shard_map/ppermute | solution.py:281
  21.4 0.0 collective-permute-done.2.refs_1_
  21.4 3.6 %collective-permute-done.1.refs_0_ = bf16[1056,128]{1,0:T(8,128)(2,1)S(1)} collective-permute-done((bf16[1056,128]{1,0:T(8,128)(2,1)}, bf16[1056,128]{1,0:T(8,128)(2,1)S(1)}, u32[]{:S(2)}, u32[]{:S(2)}) %collective-permute-start.1) | collective-permute-done | bytes 270368 | tf_op jit(solution)/shard_map/ppermute | solution.py:281
  25.0 0.4 carry.1
  25.4 0.1 collective-permute-start.4
  25.5 1.5 collective-permute-done.4.got_ref
  27.0 0.0 copy-done
  27.0 0.0 copy-done.4
  27.0 0.0 copy-done.5
  27.0 0.0 copy-done.6
  27.0 0.0 copy-start.3
  27.1 3.1 %finish.1 = (f32[256,2048]{1,0:T(8,128)S(1)}, bf16[768,2048]{1,0:T(8,128)(2,1)S(1)}) custom-call(s32[1]{0:T(128)} %bitcast.half_ref.core_ref, f32[2,256,1024]{2,1,0:T(8,128)S(1)} %get-tuple-element.30.intra_ref, bf16[256,2048]{1,0:T(8,128)(2,1)S(1)} %bitcast.28, bf16[1024,128]{1,0:T(8,128)(2,1)S(1)} %get-tuple-element.34.keep_ref, ...), custom_call_target="tpu_custom_call" | custom-call | tf_op jit(solution)/shard_map/finish/pallas_call | solution.py:28
  30.2 0.0 copy-start.1
  30.2 0.0 copy-start.2
  30.2 85.0 %all_to_all.10 = bf16[32,24,2048]{2,1,0:T(8,128)(2,1)S(1)} all-to-all(bf16[32,24,2048]{2,1,0:T(8,128)(2,1)S(1)} %bitcast.29), channel_id=1, replica_groups=mesh['seq'=8,'exp'=32] {'exp'}, dimensions={0} | all-to-all | bytes 6291456 | tf_op jit(solution)/shard_map/all_to_all | solution.py:326
  115.2 0.0 copy-done.3
  115.2 0.0 copy-done.1
  115.2 0.0 copy-done.2
  115.2 7.5 %expert.1 = bf16[768,2048]{1,0:T(8,128)(2,1)S(1)} custom-call(bf16[768,2048]{1,0:T(8,128)(2,1)S(1)} %bitcast.25, bf16[2048,768]{1,0:T(8,128)(2,1)S(1)} %bitcast.30, bf16[2048,768]{1,0:T(8,128)(2,1)S(1)} %bitcast.31, bf16[768,2048]{1,0:T(8,128)(2,1)S(1)} %bitcast.32), custom_call_target="tpu_custom_call" | custom-call | tf_op jit(solution)/shard_map/expert/pallas_call | solution.py:28
  122.7 77.9 %all_to_all.11 = bf16[32,24,2048]{2,1,0:T(8,128)(2,1)S(1)} all-to-all(bf16[32,24,2048]{2,1,0:T(8,128)(2,1)S(1)} %bitcast.26), channel_id=1, replica_groups=mesh['seq'=8,'exp'=32] {'exp'}, dimensions={0} | all-to-all | bytes 6291456 | tf_op jit(solution)/shard_map/all_to_all | solution.py:334
  200.6 1.7 combine.1
Async XLA Ops:
  2.4 13.7 %copy-start.7 = (s32[1,256,2]{1,2,0:T(2,128)S(1)}, s32[1,256,2]{1,2,0:T(2,128)}, u32[]{:S(2)}) copy-start(s32[1,256,2]{1,2,0:T(2,128)} %param.19) | copy-start | bytes 6148
  2.4 13.7 %copy-start.8 = (s32[1,256,2]{1,2,0:T(2,128)S(1)}, s32[1,256,2]{1,2,0:T(2,128)}, u32[]{:S(2)}) copy-start(s32[1,256,2]{1,2,0:T(2,128)} %param.20) | copy-start | bytes 6148
  2.4 2.6 %collective-permute-start = (bf16[1056,128]{1,0:T(8,128)(2,1)S(1)}, bf16[1056,128]{1,0:T(8,128)(2,1)S(1)}, u32[]{:S(2)}, u32[]{:S(2)}) collective-permute-start(bf16[1056,128]{1,0:T(8,128)(2,1)S(1)} %contrib.3), channel_id=1, source_target_pairs={{0,32},{32,0},{64,96},{96,64},{128,160},{160,128},{192,224},{224,1... | collective-permute-start | bytes 811016 | tf_op jit(solution)/shard_map/ppermute | solution.py:272
  5.0 22.1 %copy-start = (bf16[1,256,2048]{2,1,0:T(8,128)(2,1)S(1)}, bf16[1,256,2048]{2,1,0:T(8,128)(2,1)}, u32[]{:S(2)}) copy-start(bf16[1,256,2048]{2,1,0:T(8,128)(2,1)} %param.13) | copy-start | bytes 3145732
  5.0 22.0 %copy-start.4 = (bf16[1,256,2048]{2,1,0:T(8,128)(2,1)S(1)}, bf16[1,256,2048]{2,1,0:T(8,128)(2,1)}, u32[]{:S(2)}) copy-start(bf16[1,256,2048]{2,1,0:T(8,128)(2,1)} %param.12) | copy-start | bytes 3145732
  5.0 22.0 %copy-start.5 = (f32[2048]{0:T(1024)S(1)}, f32[2048]{0:T(1024)}, u32[]{:S(2)}) copy-start(f32[2048]{0:T(1024)} %param.17) | copy-start | bytes 24580
  5.0 22.0 %copy-start.6 = (f32[2048]{0:T(1024)S(1)}, f32[2048]{0:T(1024)}, u32[]{:S(2)}) copy-start(f32[2048]{0:T(1024)} %param.18) | copy-start | bytes 24580
  5.9 15.5 %collective-permute-start.3 = (bf16[1056,128]{1,0:T(8,128)(2,1)}, bf16[1056,128]{1,0:T(8,128)(2,1)S(1)}, u32[]{:S(2)}, u32[]{:S(2)}) collective-permute-start(bf16[1056,128]{1,0:T(8,128)(2,1)} %pair.1), channel_id=1, source_target_pairs={{0,192},{32,224},{64,0},{96,32},{128,64},{160,96},{192,128},{224,1... | collective-permute-start | bytes 811016 | tf_op jit(solution)/shard_map/ppermute | solution.py:281
  8.9 12.5 %collective-permute-start.2 = (bf16[1056,128]{1,0:T(8,128)(2,1)}, bf16[1056,128]{1,0:T(8,128)(2,1)S(1)}, u32[]{:S(2)}, u32[]{:S(2)}) collective-permute-start(bf16[1056,128]{1,0:T(8,128)(2,1)} %pair.1), channel_id=1, source_target_pairs={{0,128},{32,160},{64,192},{96,224},{128,0},{160,32},{192,64},{224,... | collective-permute-start | bytes 811016 | tf_op jit(solution)/shard_map/ppermute | solution.py:281
  9.5 15.5 %collective-permute-start.1 = (bf16[1056,128]{1,0:T(8,128)(2,1)}, bf16[1056,128]{1,0:T(8,128)(2,1)S(1)}, u32[]{:S(2)}, u32[]{:S(2)}) collective-permute-start(bf16[1056,128]{1,0:T(8,128)(2,1)} %pair.1), channel_id=1, source_target_pairs={{0,64},{32,96},{64,128},{96,160},{128,192},{160,224},{192,0},{224,... | collective-permute-start | bytes 811016 | tf_op jit(solution)/shard_map/ppermute | solution.py:281
  25.4 1.6 collective-permute-start.4
  27.0 88.1 %copy-start.3 = (bf16[1,768,2048]{2,1,0:T(8,128)(2,1)S(1)}, bf16[1,768,2048]{2,1,0:T(8,128)(2,1)}, u32[]{:S(2)}) copy-start(bf16[1,768,2048]{2,1,0:T(8,128)(2,1)} %param.23) | copy-start | bytes 9437188
  30.2 85.0 %copy-start.1 = (bf16[1,2048,768]{2,1,0:T(8,128)(2,1)S(1)}, bf16[1,2048,768]{2,1,0:T(8,128)(2,1)}, u32[]{:S(2)}) copy-start(bf16[1,2048,768]{2,1,0:T(8,128)(2,1)} %param.21) | copy-start | bytes 9437188
  30.2 85.0 %copy-start.2 = (bf16[1,2048,768]{2,1,0:T(8,128)(2,1)S(1)}, bf16[1,2048,768]{2,1,0:T(8,128)(2,1)}, u32[]{:S(2)}) copy-start(bf16[1,2048,768]{2,1,0:T(8,128)(2,1)} %param.22) | copy-start | bytes 9437188

commit v5 on v4

--- a/solution.py
+++ b/solution.py
@@ -167,29 +167,45 @@
     mix_ref[...] = jnp.where(used, dot(level, spread, 0, 0) * (1.0 / 256.0), 0.0).astype(BF16)
 
 
-def finish_body(
-    core_ref, intra_ref, q_ref, keep_ref, got_ref, grow_ref, x_ref, attn_gain_ref, norm_gain_ref, pick_ref, h_ref, send_ref
-):
-    block, width = q_ref.shape
-    per = grow_ref.shape[2]
-    heads = 2 * per
+def some_heads(half, intra_ref, q_ref, state_ref, grow_ref, x_ref, gain_ref, h_ref, squares_ref):
+    heads = grow_ref.shape[2]
+    block, width = h_ref.shape
     dh = width // heads
-    core = core_ref[0]
+    grow = grow_ref[half]
     squares = jnp.zeros((block, dh), F32)
     for h in range(heads):
         cols = slice(h * dh, (h + 1) * dh)
-        rows = slice(h % per * dh, (h % per + 1) * dh)
-        state = jnp.where(core == h // per, keep_ref[rows, :].astype(F32), got_ref[rows, :].astype(F32))
-        raw = intra_ref[h // per, :, rows] + grow_ref[h // per, :, h % per : h % per + 1] * dot(q_ref[:, cols], state.astype(BF16))
+        all_cols = pl.ds(pl.multiple_of(half * width + h * dh, dh), dh)
+        raw = intra_ref[half, :, cols] + grow[:, h : h + 1] * dot(q_ref[:, all_cols], state_ref[cols, :])
         scale = lax.rsqrt(jnp.mean(raw * raw, axis=-1, keepdims=True) + 1e-06)
-        res = x_ref[:, cols].astype(F32) + attn_gain_ref[:, cols] * (raw * scale)
+        res = x_ref[:, all_cols].astype(F32) + gain_ref[:, all_cols] * (raw * scale)
         h_ref[:, cols] = res
         squares = squares + res * res
+    squares_ref[...] = squares
+
+
+def heads_body(half_ref, *refs):
+    some_heads(half_ref[0], *refs)
+
+
+def finish_body(
+    core_ref, intra_ref, q_ref, got_ref, grow_ref, x_ref, attn_gain_ref, norm_gain_ref, pick_ref, own_ref, squares_ref,
+    h_ref, send_ref, rest_ref, more_ref
+):
+    block, width = h_ref.shape
+    half = width // 2
+    core = core_ref[0]
+    some_heads(1 - core, intra_ref, q_ref, got_ref, grow_ref, x_ref, attn_gain_ref, rest_ref, more_ref)
+    squares = squares_ref[...] + more_ref[...]
     scale = lax.rsqrt(jnp.sum(squares, axis=-1, keepdims=True) / width + 1e-06)
     step = 512
     for c in range(0, width, step):
         cols = slice(c, c + step)
-        normed = (norm_gain_ref[:, cols] * h_ref[:, cols] * scale).astype(BF16)
+        from_half = slice(c % half, c % half + step)
+        is_own = core == c // half
+        res = jnp.where(is_own, own_ref[:, from_half], rest_ref[:, from_half])
+        h_ref[:, cols] = res
+        normed = (norm_gain_ref[:, cols] * res * scale).astype(BF16)
         send_ref[:, cols] = dot(pick_ref[...], normed).astype(BF16)
 
 
@@ -277,10 +293,10 @@
 def of_earlier_chips(pair):
     blocks = lax.axis_size("seq")
     chips = blocks // 2
-    return [
-        lax.ppermute(pair, "seq", [(i, (i // 2 + by) % chips * 2 + i % 2) for i in range(blocks)])
-        for by in range(1, chips)
-    ]
+    return {
+        by: lax.ppermute(pair, "seq", [(i, (i // 2 + by) % chips * 2 + i % 2) for i in range(blocks)])
+        for by in sorted(range(1, chips), key=lambda by: min(by, chips - by))
+    }
 
 
 def carried_states(own, other, earlier, core, chip):
@@ -314,14 +330,22 @@
         ids.T,
         gate_levels[0].T,
     )
-    earlier, intra, grow, pick, mix = lax.optimization_barrier((earlier, intra, grow, pick, mix))
-    keep, got = carried_states(own, other, earlier, core, chip)
+    *states, intra, grow, pick, mix = lax.optimization_barrier((*earlier.values(), intra, grow, pick, mix))
+    earlier = dict(zip(earlier, states))
+    keep, got = carried_states(own, other, [earlier[by] for by in sorted(earlier)], core, chip)
+    common = (grow, x, attn_gain[None])
+    half = (block, width // 2)
+    per_row = (block, width // heads)
+    own_res, squares = local(
+        heads_body, "heads", [(half, F32), (per_row, F32)], intra, q, keep, *common, scalars=(core,)
+    )
     h_res, send = local(
         finish_body,
         "finish",
         [((block, width), F32), ((slots, width), BF16)],
-        *(intra, q, keep, got, grow, x, attn_gain[None], norm_gain[None], pick),
+        *(intra, q, got, *common, norm_gain[None], pick, own_res, squares),
         scalars=(core,),
+        scratch=[pltpu.VMEM(half, F32), pltpu.VMEM(per_row, F32)],
     )
     arrived = lax.all_to_all(send.reshape(experts, cap, width), "exp", 0, 0, tiled=True)
     done = local(

time: 203 us -> 200 us (0.985)
  waiting for transfers between devices: 9.81 us -> 5.74 us
    ppermute x3, waiting for transfers between devices: 8.29 us -> 5.32 us  [of_earlier_chips(): lax.ppermute(pair, 'seq', [(i, (i // 2 + by) % chips * 2 + i % 2) for i i...]
    pallas_call x5 -> x6, Pallas kernels: 12.5 us -> 12.6 us  [local(): pl.pallas_call(body, out_shape=tuple((pltpu.VMEM(shape, dtype) for shape,...]
  transfers between devices with their start and end apart: 5 -> 5, of which waited for: 3 -> 2; matrix products, arithmetic and copies ran while one was open for 0% -> 0% of each run, Pallas kernels for 4% -> 5%
where the time goes in v5:
time: 200 us; the launch traced here: 199 us
  blocking collectives  163 us (82%)
  Pallas kernels  24.7 us (12%)
  waiting for transfers between devices  5.74 us (3%)
  starting transfers between devices  5.41 us (3%)
    all_to_all x1, blocking collectives, per_device(): lax.all_to_all(send.reshape(experts, cap, width), 'exp', 0, 0, tiled=True)  85 us
    all_to_all x1, blocking collectives, per_device(): lax.all_to_all(done.reshape(experts, cap, width), 'exp', 0, 0, tiled=True)  77.9 us
    pallas_call x6, Pallas kernels, local(): pl.pallas_call(body, out_shape=tuple((pltpu.VMEM(shape, dtype) for shape,...  12.6 us
    pallas_call x1, Pallas kernels, inside_block(): pl.pallas_call(intra_body, out_shape=(pltpu.VMEM((2, block, width // 2),...  5.55 us
    ppermute x3, waiting for transfers between devices, of_earlier_chips(): lax.ppermute(pair, 'seq', [(i, (i // 2 + by) % chips * 2 + i % 2) for i i...  5.32 us
    ppermute x3, starting transfers between devices, of_earlier_chips(): lax.ppermute(pair, 'seq', [(i, (i // 2 + by) % chips * 2 + i % 2) for i i...  5.22 us
    pallas_call x2, Pallas kernels, contribution(): pl.pallas_call(contrib_body, out_shape=pltpu.VMEM((width // 2 + LOG_ROWS,...  4.83 us
  transfers between devices with their start and end apart: 5, of which 2 were waited for; matrix products, arithmetic and copies ran while one was open for 0% of the time, Pallas kernels for 5%

profile of v5, /device:TPU:32, one launch (start us, length us, event | category | flops | bytes accessed | tf_op | source)
XLA Modules:
  0.0 199.2 jit_solution(15711187407126312499)
XLA Ops:
  0.0 2.4 %contrib.3 = bf16[1056,128]{1,0:T(8,128)(2,1)S(1)} custom-call(s32[1]{0:T(128)S(6)} %sub.3.half_ref, bf16[256,2048]{1,0:T(8,128)(2,1)} %bitcast.41, bf16[256,2048]{1,0:T(8,128)(2,1)} %bitcast.44, f32[16,256]{1,0:T(8,128)} %bitcast.47), custom_call_target="tpu_custom_call" | custom-call | tf_op jit(solution)/shard_map/contrib/pallas_call | solution.py:256
  2.4 0.0 copy-start.7
  2.4 0.0 copy-start.8
  2.4 0.1 collective-permute-start
  2.5 2.4 %contrib.2.own_ref = bf16[1056,128]{1,0:T(8,128)(2,1)S(1)} custom-call(s32[1]{0:T(128)} %bitcast.half_ref.core_ref, bf16[256,2048]{1,0:T(8,128)(2,1)} %bitcast.42, bf16[256,2048]{1,0:T(8,128)(2,1)} %bitcast.45, f32[16,256]{1,0:T(8,128)} %bitcast.48), custom_call_target="tpu_custom_call" | custom-call | tf_op jit(solution)/shard_map/contrib/pallas_call | solution.py:256
  5.0 0.0 copy-start
  5.0 0.0 copy-start.1
  5.0 0.0 copy-start.5
  5.0 0.0 collective-permute-done.other_ref
  5.0 0.9 pair.1
  5.9 3.2 %collective-permute-start.3 = (bf16[1056,128]{1,0:T(8,128)(2,1)}, bf16[1056,128]{1,0:T(8,128)(2,1)S(1)}, u32[]{:S(2)}, u32[]{:S(2)}) collective-permute-start(bf16[1056,128]{1,0:T(8,128)(2,1)} %pair.1), channel_id=1, source_target_pairs={{0,128},{32,160},{64,192},{96,224},{128,0},{160,32},{192,64},{224,... | collective-permute-start | bytes 811016 | tf_op jit(solution)/shard_map/ppermute | solution.py:297
  9.1 1.1 collective-permute-start.2
  10.1 1.0 collective-permute-start.1
  11.1 5.5 %intra.1 = (f32[2,256,1024]{2,1,0:T(8,128)S(1)}, f32[2,256,8]{2,1,0:T(8,128)S(1)}) custom-call(bf16[256,2048]{1,0:T(8,128)(2,1)} %bitcast.27, bf16[256,2048]{1,0:T(8,128)(2,1)} %bitcast.43, bf16[256,2048]{1,0:T(8,128)(2,1)} %bitcast.46, f32[16,256]{1,0:T(8,128)} %bitcast.49), custom_call_target="tpu_custom_call" | custom-call | tf_op jit(solution)/shard_map/intra/pallas_call | solution.py:275
  16.7 0.0 copy-start.6
  16.7 0.0 copy-done.7
  16.7 0.0 copy-done.8
  16.7 0.6 route.1
  17.3 0.0 collective-permute-done.3.refs_1_
  17.3 5.3 %collective-permute-done.2.refs_2_ = bf16[1056,128]{1,0:T(8,128)(2,1)S(1)} collective-permute-done((bf16[1056,128]{1,0:T(8,128)(2,1)}, bf16[1056,128]{1,0:T(8,128)(2,1)S(1)}, u32[]{:S(2)}, u32[]{:S(2)}) %collective-permute-start.2) | collective-permute-done | bytes 270368 | tf_op jit(solution)/shard_map/ppermute | solution.py:297
  22.7 0.0 collective-permute-done.1.refs_0_
  22.7 0.4 carry.1
  23.0 0.1 collective-permute-start.4
  23.1 0.0 copy-done
  23.2 0.0 copy-done.1
  23.2 0.0 copy-done.5
  23.2 1.1 heads.1
  24.3 0.4 collective-permute-done.4.got_ref
  24.7 0.0 copy-done.6
  24.7 0.0 copy-start.4
  24.7 2.1 %finish.1 = (f32[256,2048]{1,0:T(8,128)S(1)}, bf16[768,2048]{1,0:T(8,128)(2,1)S(1)}) custom-call(s32[1]{0:T(128)} %bitcast.half_ref.core_ref, f32[2,256,1024]{2,1,0:T(8,128)S(1)} %get-tuple-element.32.refs_0_.intra_ref, bf16[256,2048]{1,0:T(8,128)(2,1)S(1)} %bitcast.29, bf16[1024,128]{1,0:T(8,128)(2,1)S(1)} %collective-permute-done.4.got_ref, ...), custom_call_target="tpu_custom_call" | custom-call | tf_op jit(solution)/shard_map/finish/pallas_call | solution.py:28
  26.8 0.0 copy-start.2
  26.8 0.0 copy-start.3
  26.9 85.0 %all_to_all.10 = bf16[32,24,2048]{2,1,0:T(8,128)(2,1)S(1)} all-to-all(bf16[32,24,2048]{2,1,0:T(8,128)(2,1)S(1)} %bitcast.32), channel_id=1, replica_groups=mesh['seq'=8,'exp'=32] {'exp'}, dimensions={0} | all-to-all | bytes 6291456 | tf_op jit(solution)/shard_map/all_to_all | solution.py:350
  111.8 0.0 copy-done.4
  111.8 0.0 copy-done.2
  111.8 0.0 copy-done.3
  111.8 7.5 %expert.1 = bf16[768,2048]{1,0:T(8,128)(2,1)S(1)} custom-call(bf16[768,2048]{1,0:T(8,128)(2,1)S(1)} %bitcast.25, bf16[2048,768]{1,0:T(8,128)(2,1)S(1)} %bitcast.33, bf16[2048,768]{1,0:T(8,128)(2,1)S(1)} %bitcast.34, bf16[768,2048]{1,0:T(8,128)(2,1)S(1)} %bitcast.35), custom_call_target="tpu_custom_call" | custom-call | tf_op jit(solution)/shard_map/expert/pallas_call | solution.py:28
  119.3 77.9 %all_to_all.11 = bf16[32,24,2048]{2,1,0:T(8,128)(2,1)S(1)} all-to-all(bf16[32,24,2048]{2,1,0:T(8,128)(2,1)S(1)} %bitcast.26), channel_id=1, replica_groups=mesh['seq'=8,'exp'=32] {'exp'}, dimensions={0} | all-to-all | bytes 6291456 | tf_op jit(solution)/shard_map/all_to_all | solution.py:358
  197.3 1.8 combine.1
Async XLA Ops:
  2.4 14.3 %copy-start.7 = (s32[1,256,2]{1,2,0:T(2,128)S(1)}, s32[1,256,2]{1,2,0:T(2,128)}, u32[]{:S(2)}) copy-start(s32[1,256,2]{1,2,0:T(2,128)} %param.19) | copy-start | bytes 6148
  2.4 14.3 %copy-start.8 = (s32[1,256,2]{1,2,0:T(2,128)S(1)}, s32[1,256,2]{1,2,0:T(2,128)}, u32[]{:S(2)}) copy-start(s32[1,256,2]{1,2,0:T(2,128)} %param.20) | copy-start | bytes 6148
  2.4 2.6 %collective-permute-start = (bf16[1056,128]{1,0:T(8,128)(2,1)S(1)}, bf16[1056,128]{1,0:T(8,128)(2,1)S(1)}, u32[]{:S(2)}, u32[]{:S(2)}) collective-permute-start(bf16[1056,128]{1,0:T(8,128)(2,1)S(1)} %contrib.3), channel_id=1, source_target_pairs={{0,32},{32,0},{64,96},{96,64},{128,160},{160,128},{192,224},{224,1... | collective-permute-start | bytes 811016 | tf_op jit(solution)/shard_map/ppermute | solution.py:288
  5.0 18.2 %copy-start = (bf16[1,256,2048]{2,1,0:T(8,128)(2,1)S(1)}, bf16[1,256,2048]{2,1,0:T(8,128)(2,1)}, u32[]{:S(2)}) copy-start(bf16[1,256,2048]{2,1,0:T(8,128)(2,1)} %param.13) | copy-start | bytes 3145732
  5.0 18.2 %copy-start.1 = (bf16[1,256,2048]{2,1,0:T(8,128)(2,1)S(1)}, bf16[1,256,2048]{2,1,0:T(8,128)(2,1)}, u32[]{:S(2)}) copy-start(bf16[1,256,2048]{2,1,0:T(8,128)(2,1)} %param.12) | copy-start | bytes 3145732
  5.0 18.2 %copy-start.5 = (f32[2048]{0:T(1024)S(1)}, f32[2048]{0:T(1024)}, u32[]{:S(2)}) copy-start(f32[2048]{0:T(1024)} %param.17) | copy-start | bytes 24580
  5.9 11.4 %collective-permute-start.3 = (bf16[1056,128]{1,0:T(8,128)(2,1)}, bf16[1056,128]{1,0:T(8,128)(2,1)S(1)}, u32[]{:S(2)}, u32[]{:S(2)}) collective-permute-start(bf16[1056,128]{1,0:T(8,128)(2,1)} %pair.1), channel_id=1, source_target_pairs={{0,128},{32,160},{64,192},{96,224},{128,0},{160,32},{192,64},{224,... | collective-permute-start | bytes 811016 | tf_op jit(solution)/shard_map/ppermute | solution.py:297
  9.1 13.6 %collective-permute-start.2 = (bf16[1056,128]{1,0:T(8,128)(2,1)}, bf16[1056,128]{1,0:T(8,128)(2,1)S(1)}, u32[]{:S(2)}, u32[]{:S(2)}) collective-permute-start(bf16[1056,128]{1,0:T(8,128)(2,1)} %pair.1), channel_id=1, source_target_pairs={{0,192},{32,224},{64,0},{96,32},{128,64},{160,96},{192,128},{224,1... | collective-permute-start | bytes 811016 | tf_op jit(solution)/shard_map/ppermute | solution.py:297
  10.1 12.5 %collective-permute-start.1 = (bf16[1056,128]{1,0:T(8,128)(2,1)}, bf16[1056,128]{1,0:T(8,128)(2,1)S(1)}, u32[]{:S(2)}, u32[]{:S(2)}) collective-permute-start(bf16[1056,128]{1,0:T(8,128)(2,1)} %pair.1), channel_id=1, source_target_pairs={{0,64},{32,96},{64,128},{96,160},{128,192},{160,224},{192,0},{224,... | collective-permute-start | bytes 811016 | tf_op jit(solution)/shard_map/ppermute | solution.py:297
  16.7 8.0 %copy-start.6 = (f32[2048]{0:T(1024)S(1)}, f32[2048]{0:T(1024)}, u32[]{:S(2)}) copy-start(f32[2048]{0:T(1024)} %param.18) | copy-start | bytes 24580
  23.0 1.6 collective-permute-start.4
  24.7 87.2 %copy-start.4 = (bf16[1,768,2048]{2,1,0:T(8,128)(2,1)S(1)}, bf16[1,768,2048]{2,1,0:T(8,128)(2,1)}, u32[]{:S(2)}) copy-start(bf16[1,768,2048]{2,1,0:T(8,128)(2,1)} %param.23) | copy-start | bytes 9437188
  26.8 85.0 %copy-start.2 = (bf16[1,2048,768]{2,1,0:T(8,128)(2,1)S(1)}, bf16[1,2048,768]{2,1,0:T(8,128)(2,1)}, u32[]{:S(2)}) copy-start(bf16[1,2048,768]{2,1,0:T(8,128)(2,1)} %param.21) | copy-start | bytes 9437188
  26.8 85.0 %copy-start.3 = (bf16[1,2048,768]{2,1,0:T(8,128)(2,1)S(1)}, bf16[1,2048,768]{2,1,0:T(8,128)(2,1)}, u32[]{:S(2)}) copy-start(bf16[1,2048,768]{2,1,0:T(8,128)(2,1)} %param.22) | copy-start | bytes 9437188

commit v6 on v5

--- a/solution.py
+++ b/solution.py
@@ -92,6 +92,24 @@
         kw = (k_ref[:, cols].astype(F32) * weight).astype(BF16)
         rows = pl.ds(pl.multiple_of((step * per + i) * dh, dh), dh)
         out_ref[rows, :] = dot(kw, v_ref[:, cols], 0, 0).astype(BF16)
+
+
+def first_contrib_body(half_ref, k_ref, v_ref, decay_ref, all_k_ref, all_v_ref, out_ref, k_out, v_out, decayed_ref, sems):
+    width = k_out.shape[1]
+    cols = pl.ds(pl.multiple_of((1 - half_ref[0]) * width, 128), width)
+    loads = [
+        pltpu.make_async_copy(ref.at[:, cols], out, sems.at[i])
+        for i, (ref, out) in enumerate(((all_k_ref, k_out), (all_v_ref, v_out)))
+    ]
+    for load in loads:
+        load.start()
+    contrib_body(half_ref, k_ref, v_ref, decay_ref, out_ref, decayed_ref)
+    for load in loads:
+        load.wait()
+
+
+def second_contrib_body(half_ref, k_ref, v_ref, decay_ref, out_ref, decayed_ref):
+    contrib_body(half_ref, k_ref, v_ref, decay_ref, out_ref, decayed_ref)
 
 
 def pair_body(core_ref, own_ref, other_ref, out_ref):
@@ -248,24 +266,48 @@
     )(near(back), near(h_res), near(mix))
 
 
-def contribution(half, k, v, decay_t, steps=1):
+def contributions(core, k, v, decay_t):
     heads, block = decay_t.shape
-    width = k.shape[1]
-    dh = width // heads
-    columns = pl.BlockSpec((block, width // 2 // steps), lambda i, half: (0, half[0] * steps + i))
-    return pl.pallas_call(
-        contrib_body,
-        out_shape=pltpu.VMEM((width // 2 + LOG_ROWS, dh), BF16),
+    width = k.shape[1] // 2
+    dh = width // (heads // 2)
+    columns = pl.BlockSpec((block, width), lambda i, half: (0, half[0]))
+    rates = pl.BlockSpec((heads // 2, block), lambda i, half: (half[0], 0))
+    states = pltpu.VMEM((width + LOG_ROWS, dh), BF16)
+    decayed = pltpu.VMEM((block, heads // 2), F32)
+    in_hbm = pl.BlockSpec(memory_space=pltpu.HBM)
+    params = pltpu.CompilerParams(vmem_limit_bytes=VMEM_LIMIT)
+    kept = pltpu.VMEM((block, width), BF16)
+    k, v, decay_t = far(k), far(v), far(decay_t)
+    first, k_own, v_own = pl.pallas_call(
+        first_contrib_body,
+        out_shape=(states, kept, kept),
         grid_spec=pltpu.PrefetchScalarGridSpec(
             num_scalar_prefetch=1,
-            grid=(steps,),
-            in_specs=[columns, columns, pl.BlockSpec((heads // 2, block), lambda i, half: (half[0], 0))],
-            out_specs=VMEM_SPEC,
-            scratch_shapes=[pltpu.VMEM((block, heads // 2), F32)],
+            grid=(1,),
+            in_specs=[columns, columns, rates, in_hbm, in_hbm],
+            out_specs=(VMEM_SPEC,) * 3,
+            scratch_shapes=[decayed, pltpu.SemaphoreType.DMA((2,))],
         ),
-        compiler_params=pltpu.CompilerParams(vmem_limit_bytes=VMEM_LIMIT),
+        compiler_params=params,
         name="contrib",
-    )(half, far(k), far(v), far(decay_t))
+    )(1 - core, k, v, decay_t, k, v)
+
+    def second():
+        return pl.pallas_call(
+            second_contrib_body,
+            out_shape=states,
+            grid_spec=pltpu.PrefetchScalarGridSpec(
+                num_scalar_prefetch=1,
+                grid=(1,),
+                in_specs=[VMEM_SPEC, VMEM_SPEC, rates],
+                out_specs=VMEM_SPEC,
+                scratch_shapes=[decayed],
+            ),
+            compiler_params=params,
+            name="contrib",
+        )(core, near(k_own), near(v_own), decay_t)
+
+    return first, second
 
 
 def inside_block(q, k, v, decay_t):
@@ -285,8 +327,9 @@
 
 def pair_states(k, v, decay_t, core):
     swap = [(i, i ^ 1) for i in range(lax.axis_size("seq"))]
-    other = lax.ppermute(contribution(1 - core, k, v, decay_t), "seq", swap)
-    own = contribution(core, k, v, decay_t)
+    first, second = contributions(core, k, v, decay_t)
+    other = lax.ppermute(first, "seq", swap)
+    own = second()
     return own, other, local(pair_body, "pair", [(own.shape, BF16)], own, other, scalars=(core,))
 
 
@@ -295,7 +338,7 @@
     chips = blocks // 2
     return {
         by: lax.ppermute(pair, "seq", [(i, (i // 2 + by) % chips * 2 + i % 2) for i in range(blocks)])
-        for by in sorted(range(1, chips), key=lambda by: min(by, chips - by))
+        for by in sorted(range(1, chips), key=lambda by: (min(by, chips - by), -by))
     }
 
 

time: 200 us -> 199 us (level)
  transfers between devices with their start and end apart: 5 -> 5, of which waited for: 2 -> 3; matrix products, arithmetic and copies ran while one was open for 0% -> 0% of each run, Pallas kernels for 5% -> 5%
where the time goes in v6:
time: 199 us
  blocking collectives  163 us (82%)
  Pallas kernels  24.4 us (12%)
  starting transfers between devices  6.62 us (3%)
  waiting for transfers between devices  4.5 us (2%)
    all_to_all x1, blocking collectives, per_device(): lax.all_to_all(send.reshape(experts, cap, width), 'exp', 0, 0, tiled=True)  85 us
    all_to_all x1, blocking collectives, per_device(): lax.all_to_all(done.reshape(experts, cap, width), 'exp', 0, 0, tiled=True)  77.9 us
    pallas_call x6, Pallas kernels, local(): pl.pallas_call(body, out_shape=tuple((pltpu.VMEM(shape, dtype) for shape,...  12.6 us
    ppermute x3, starting transfers between devices, of_earlier_chips(): lax.ppermute(pair, 'seq', [(i, (i // 2 + by) % chips * 2 + i % 2) for i i...  6.43 us
    pallas_call x1, Pallas kernels, inside_block(): pl.pallas_call(intra_body, out_shape=(pltpu.VMEM((2, block, width // 2),...  5.54 us
    ppermute x3, waiting for transfers between devices, of_earlier_chips(): lax.ppermute(pair, 'seq', [(i, (i // 2 + by) % chips * 2 + i % 2) for i i...  4.08 us
  transfers between devices with their start and end apart: 5, of which 3 were waited for; matrix products, arithmetic and copies ran while one was open for 0% of the time, Pallas kernels for 5%

profile of v6, /device:TPU:32, one launch (start us, length us, event | category | flops | bytes accessed | tf_op | source)
XLA Modules:
  0.0 198.8 jit_solution(14265345229836362406)
XLA Ops:
  0.0 2.4 %contrib.2 = (bf16[1056,128]{1,0:T(8,128)(2,1)S(1)}, bf16[256,1024]{1,0:T(8,128)(2,1)S(1)}, bf16[256,1024]{1,0:T(8,128)(2,1)S(1)}) custom-call(s32[1]{0:T(128)S(6)} %sub.3.half_ref, bf16[256,2048]{1,0:T(8,128)(2,1)} %bitcast.41, bf16[256,2048]{1,0:T(8,128)(2,1)} %bitcast.44, f32[16,256]{1,0:T(8,128)} %bitcast.47, bf16[256,2048]{1,0:T(8,128)(2,1)} %bitcast.42, ...), custom_call_target="tpu_custom_call" | custom-call | tf_op jit(solution)/shard_map/contrib/pallas_call | solution.py:281
  2.4 0.0 copy-start.7
  2.5 0.0 copy-start.8
  2.5 0.1 collective-permute-start
  2.6 0.0 copy-start
  2.6 0.0 copy-start.1
  2.6 0.0 copy-start.5
  2.6 2.1 %contrib.3.own_ref = bf16[1056,128]{1,0:T(8,128)(2,1)S(1)} custom-call(s32[1]{0:T(128)} %bitcast.half_ref.core_ref, bf16[256,1024]{1,0:T(8,128)(2,1)S(1)} %get-tuple-element.28.k_ref, bf16[256,1024]{1,0:T(8,128)(2,1)S(1)} %get-tuple-element.29.v_ref, f32[16,256]{1,0:T(8,128)} %bitcast.48), custom_call_target="tpu_custom_call" | custom-call | tf_op jit(solution)/shard_map/contrib/pallas_call | solution.py:296
  4.7 0.0 collective-permute-done.other_ref
  4.7 0.9 pair.1
  5.6 3.2 %collective-permute-start.3 = (bf16[1056,128]{1,0:T(8,128)(2,1)}, bf16[1056,128]{1,0:T(8,128)(2,1)S(1)}, u32[]{:S(2)}, u32[]{:S(2)}) collective-permute-start(bf16[1056,128]{1,0:T(8,128)(2,1)} %pair.1), channel_id=1, source_target_pairs={{0,128},{32,160},{64,192},{96,224},{128,0},{160,32},{192,64},{224,... | collective-permute-start | bytes 811016 | tf_op jit(solution)/shard_map/ppermute | solution.py:340
  8.8 0.7 collective-permute-start.2
  9.4 2.6 %collective-permute-start.1 = (bf16[1056,128]{1,0:T(8,128)(2,1)}, bf16[1056,128]{1,0:T(8,128)(2,1)S(1)}, u32[]{:S(2)}, u32[]{:S(2)}) collective-permute-start(bf16[1056,128]{1,0:T(8,128)(2,1)} %pair.1), channel_id=1, source_target_pairs={{0,192},{32,224},{64,0},{96,32},{128,64},{160,96},{192,128},{224,1... | collective-permute-start | bytes 811016 | tf_op jit(solution)/shard_map/ppermute | solution.py:340
  12.0 5.5 %intra.1 = (f32[2,256,1024]{2,1,0:T(8,128)S(1)}, f32[2,256,8]{2,1,0:T(8,128)S(1)}) custom-call(bf16[256,2048]{1,0:T(8,128)(2,1)} %bitcast.27, bf16[256,2048]{1,0:T(8,128)(2,1)} %bitcast.43, bf16[256,2048]{1,0:T(8,128)(2,1)} %bitcast.46, f32[16,256]{1,0:T(8,128)} %bitcast.49), custom_call_target="tpu_custom_call" | custom-call | tf_op jit(solution)/shard_map/intra/pallas_call | solution.py:317
  17.6 0.0 copy-start.6
  17.6 0.0 copy-done.7
  17.6 0.0 copy-done.8
  17.6 0.6 route.1
  18.2 0.0 collective-permute-done.3.refs_1_
  18.2 3.7 %collective-permute-done.2.refs_0_ = bf16[1056,128]{1,0:T(8,128)(2,1)S(1)} collective-permute-done((bf16[1056,128]{1,0:T(8,128)(2,1)}, bf16[1056,128]{1,0:T(8,128)(2,1)S(1)}, u32[]{:S(2)}, u32[]{:S(2)}) %collective-permute-start.2) | collective-permute-done | bytes 270368 | tf_op jit(solution)/shard_map/ppermute | solution.py:340
  21.9 0.4 collective-permute-done.1.refs_2_
  22.3 0.4 carry.1
  22.7 0.1 collective-permute-start.4
  22.8 0.0 copy-done
  22.8 0.0 copy-done.1
  22.8 0.0 copy-done.5
  22.8 1.1 heads.1
  23.9 0.4 collective-permute-done.4.got_ref
  24.3 0.0 copy-done.6
  24.3 0.0 copy-start.4
  24.3 2.1 %finish.1 = (f32[256,2048]{1,0:T(8,128)S(1)}, bf16[768,2048]{1,0:T(8,128)(2,1)S(1)}) custom-call(s32[1]{0:T(128)} %bitcast.half_ref.core_ref, f32[2,256,1024]{2,1,0:T(8,128)S(1)} %get-tuple-element.38.refs_0_.intra_ref, bf16[256,2048]{1,0:T(8,128)(2,1)S(1)} %bitcast.29, bf16[1024,128]{1,0:T(8,128)(2,1)S(1)} %collective-permute-done.4.got_ref, ...), custom_call_target="tpu_custom_call" | custom-call | tf_op jit(solution)/shard_map/finish/pallas_call | solution.py:28
  26.5 0.0 copy-start.2
  26.5 0.0 copy-start.3
  26.5 85.0 %all_to_all.10 = bf16[32,24,2048]{2,1,0:T(8,128)(2,1)S(1)} all-to-all(bf16[32,24,2048]{2,1,0:T(8,128)(2,1)S(1)} %bitcast.32), channel_id=1, replica_groups=mesh['seq'=8,'exp'=32] {'exp'}, dimensions={0} | all-to-all | bytes 6291456 | tf_op jit(solution)/shard_map/all_to_all | solution.py:393
  111.5 0.0 copy-done.4
  111.5 0.0 copy-done.2
  111.5 0.0 copy-done.3
  111.5 7.5 %expert.1 = bf16[768,2048]{1,0:T(8,128)(2,1)S(1)} custom-call(bf16[768,2048]{1,0:T(8,128)(2,1)S(1)} %bitcast.25, bf16[2048,768]{1,0:T(8,128)(2,1)S(1)} %bitcast.33, bf16[2048,768]{1,0:T(8,128)(2,1)S(1)} %bitcast.34, bf16[768,2048]{1,0:T(8,128)(2,1)S(1)} %bitcast.35), custom_call_target="tpu_custom_call" | custom-call | tf_op jit(solution)/shard_map/expert/pallas_call | solution.py:28
  119.0 77.9 %all_to_all.11 = bf16[32,24,2048]{2,1,0:T(8,128)(2,1)S(1)} all-to-all(bf16[32,24,2048]{2,1,0:T(8,128)(2,1)S(1)} %bitcast.26), channel_id=1, replica_groups=mesh['seq'=8,'exp'=32] {'exp'}, dimensions={0} | all-to-all | bytes 6291456 | tf_op jit(solution)/shard_map/all_to_all | solution.py:401
  196.9 1.8 combine.1
Async XLA Ops:
  2.4 15.1 %copy-start.7 = (s32[1,256,2]{1,2,0:T(2,128)S(1)}, s32[1,256,2]{1,2,0:T(2,128)}, u32[]{:S(2)}) copy-start(s32[1,256,2]{1,2,0:T(2,128)} %param.19) | copy-start | bytes 6148
  2.5 15.1 %copy-start.8 = (s32[1,256,2]{1,2,0:T(2,128)S(1)}, s32[1,256,2]{1,2,0:T(2,128)}, u32[]{:S(2)}) copy-start(s32[1,256,2]{1,2,0:T(2,128)} %param.20) | copy-start | bytes 6148
  2.5 2.2 %collective-permute-start = (bf16[1056,128]{1,0:T(8,128)(2,1)S(1)}, bf16[1056,128]{1,0:T(8,128)(2,1)S(1)}, u32[]{:S(2)}, u32[]{:S(2)}) collective-permute-start(bf16[1056,128]{1,0:T(8,128)(2,1)S(1)} %get-tuple-element.30), channel_id=1, source_target_pairs={{0,32},{32,0},{64,96},{96,64},{128,160},{160,128},{192,224},{224,1... | collective-permute-start | bytes 811016 | tf_op jit(solution)/shard_map/ppermute | solution.py:331
  2.6 20.2 %copy-start = (bf16[1,256,2048]{2,1,0:T(8,128)(2,1)S(1)}, bf16[1,256,2048]{2,1,0:T(8,128)(2,1)}, u32[]{:S(2)}) copy-start(bf16[1,256,2048]{2,1,0:T(8,128)(2,1)} %param.13) | copy-start | bytes 3145732
  2.6 20.2 %copy-start.1 = (bf16[1,256,2048]{2,1,0:T(8,128)(2,1)S(1)}, bf16[1,256,2048]{2,1,0:T(8,128)(2,1)}, u32[]{:S(2)}) copy-start(bf16[1,256,2048]{2,1,0:T(8,128)(2,1)} %param.12) | copy-start | bytes 3145732
  2.6 20.2 %copy-start.5 = (f32[2048]{0:T(1024)S(1)}, f32[2048]{0:T(1024)}, u32[]{:S(2)}) copy-start(f32[2048]{0:T(1024)} %param.17) | copy-start | bytes 24580
  5.6 12.7 %collective-permute-start.3 = (bf16[1056,128]{1,0:T(8,128)(2,1)}, bf16[1056,128]{1,0:T(8,128)(2,1)S(1)}, u32[]{:S(2)}, u32[]{:S(2)}) collective-permute-start(bf16[1056,128]{1,0:T(8,128)(2,1)} %pair.1), channel_id=1, source_target_pairs={{0,128},{32,160},{64,192},{96,224},{128,0},{160,32},{192,64},{224,... | collective-permute-start | bytes 811016 | tf_op jit(solution)/shard_map/ppermute | solution.py:340
  8.8 13.2 %collective-permute-start.2 = (bf16[1056,128]{1,0:T(8,128)(2,1)}, bf16[1056,128]{1,0:T(8,128)(2,1)S(1)}, u32[]{:S(2)}, u32[]{:S(2)}) collective-permute-start(bf16[1056,128]{1,0:T(8,128)(2,1)} %pair.1), channel_id=1, source_target_pairs={{0,64},{32,96},{64,128},{96,160},{128,192},{160,224},{192,0},{224,... | collective-permute-start | bytes 811016 | tf_op jit(solution)/shard_map/ppermute | solution.py:340
  9.4 12.9 %collective-permute-start.1 = (bf16[1056,128]{1,0:T(8,128)(2,1)}, bf16[1056,128]{1,0:T(8,128)(2,1)S(1)}, u32[]{:S(2)}, u32[]{:S(2)}) collective-permute-start(bf16[1056,128]{1,0:T(8,128)(2,1)} %pair.1), channel_id=1, source_target_pairs={{0,192},{32,224},{64,0},{96,32},{128,64},{160,96},{192,128},{224,1... | collective-permute-start | bytes 811016 | tf_op jit(solution)/shard_map/ppermute | solution.py:340
  17.6 6.8 %copy-start.6 = (f32[2048]{0:T(1024)S(1)}, f32[2048]{0:T(1024)}, u32[]{:S(2)}) copy-start(f32[2048]{0:T(1024)} %param.18) | copy-start | bytes 24580
  22.7 1.6 collective-permute-start.4
  24.3 87.2 %copy-start.4 = (bf16[1,768,2048]{2,1,0:T(8,128)(2,1)S(1)}, bf16[1,768,2048]{2,1,0:T(8,128)(2,1)}, u32[]{:S(2)}) copy-start(bf16[1,768,2048]{2,1,0:T(8,128)(2,1)} %param.23) | copy-start | bytes 9437188
  26.5 85.0 %copy-start.2 = (bf16[1,2048,768]{2,1,0:T(8,128)(2,1)S(1)}, bf16[1,2048,768]{2,1,0:T(8,128)(2,1)}, u32[]{:S(2)}) copy-start(bf16[1,2048,768]{2,1,0:T(8,128)(2,1)} %param.21) | copy-start | bytes 9437188
  26.5 85.0 %copy-start.3 = (bf16[1,2048,768]{2,1,0:T(8,128)(2,1)S(1)}, bf16[1,2048,768]{2,1,0:T(8,128)(2,1)}, u32[]{:S(2)}) copy-start(bf16[1,2048,768]{2,1,0:T(8,128)(2,1)} %param.22) | copy-start | bytes 9437188
